TPU v7x, 32 devices: a whole 2x2x4 slice. The times are simulated.
32 devices in a mesh: dp: 8 (over z, core), tensor: 4 (over y, x).
Axes of the slice: x: 2, y: 2, z: 4, core: 2. Of those that a mesh axis runs over, the one named last changes fastest.
Arguments:
- inputs: bfloat16 [8, 1024, 1024], P('dp'), may hold values from -6 to 6
- cotangent: bfloat16 [8, 1024, 1024], P('dp'), may hold values from -6 to 6
- groups: int32 [8], P('dp'), may hold values from 0 to 7
- counts: int32 [8], replicated, may hold values from 128 to 512
- vector_parameters: float32 [6, 1024], replicated, may hold values from -0.9 to 1.4, as said below
- query_value_bias: float32 [2, 1024], P(None, 'tensor'), may hold values from -1.8 to 1.8
- hidden_bias: float32 [4096], P('tensor'), may hold values from -1.8 to 1.8
- query_key_value_weight: bfloat16 [3, 1024, 1024], P(None, None, 'tensor'), may hold values from -0.1875 to 0.1875
- attention_output_weight: bfloat16 [1024, 1024], P('tensor'), may hold values from -0.75 to 0.75
- hidden_weight: bfloat16 [1024, 4096], P(None, 'tensor'), may hold values from -0.1875 to 0.1875
- hidden_output_weight: bfloat16 [4096, 1024], P('tensor'), may hold values from -0.09375 to 0.09375
- adapter_down: float32 [2, 1024, 4], replicated, may hold values from -0.1875 to 0.1875
- adapter_up: float32 [2, 4, 1024], replicated, may hold values from -0.18 to 0.18
- momentum_down: float32 [2, 1024, 4], replicated, may hold values from -0.039774757 to 0.039774757
- momentum_up: float32 [2, 4, 1024], replicated, may hold values from -0.079549514 to 0.079549514
- average_down: float32 [2, 1024, 4], replicated, may hold values from -0.1875 to 0.1875
- average_up: float32 [2, 4, 1024], replicated, may hold values from -0.18 to 0.18
Outputs:
- block_out: bfloat16 [8, 1024, 1024], P('dp')
- input_grad: bfloat16 [8, 1024, 1024], P('dp')
- down_gradient: float32 [2, 1024, 4], replicated
- up_gradient: float32 [2, 4, 1024], replicated
- updated_momentum_down: float32 [2, 1024, 4], replicated
- updated_momentum_up: float32 [2, 4, 1024], replicated
- updated_down: float32 [2, 1024, 4], replicated
- updated_up: float32 [2, 4, 1024], replicated
- updated_average_down: float32 [2, 1024, 4], replicated
- updated_average_up: float32 [2, 4, 1024], replicated
- copy_a: bfloat16 [2, 1024, 4], replicated
- copy_b: bfloat16 [2, 4, 1024], replicated
Inputs may be any that keep to these rules, and one draw needn't show every extreme that they name: `vector_parameters`: rows 0 and 2 are gains, the other rows shifts and biases.
All inputs are finite; a program needn't handle non-finite values.
Results may differ from a plain program's by a relative error of at most 0.018.
Values may be sent and summed in bfloat16 or wider, within the bound.
No kernel may reach another device: no remote copies, remote signals or barrier semaphores. Data moves between devices by JAX's collectives and lax.ppermute only.
A program may use at most 128 MiB of HBM per device.

v0:
```python
import functools
import math

import jax
import jax.numpy as jnp
from jax import lax
from jax.experimental import pallas as pl
from jax.experimental.pallas import tpu as pltpu
from jax.sharding import PartitionSpec as P


HEAD = 64


NORM_EPS = 1e-05
ADAPTER_SCALE = 8.0
MASK_FILL = -1e30
MOMENTUM_FACTOR = 0.9
AVERAGE_KEEP = 0.8
RATE_BASE = 0.025
WEIGHT_DECAY = 0.005
COUNT_BASE = 256.0


def layer_norm(value_rows, norm_gain, norm_bias):
    center = value_rows - jnp.mean(value_rows, axis=-1, keepdims=True)
    spread = jnp.mean(center * center, axis=-1, keepdims=True)
    return center * lax.rsqrt(spread + NORM_EPS) * norm_gain + norm_bias


def norm_back(value_rows, norm_gain, norm_bias, upstream):

    def local_norm(operand):
        return layer_norm(operand, norm_gain, norm_bias)

    _, backward_map = jax.vjp(local_norm, value_rows)
    return backward_map(upstream)[0]


def gelu_back(preact, upstream):

    def activate(operand):
        return jax.nn.gelu(operand, approximate=True)

    _, backward_map = jax.vjp(activate, preact)
    return backward_map(upstream)[0]


def to_heads(matrix, seq_count, length):
    return matrix.reshape(seq_count, length, -1, HEAD).transpose(0, 2, 1, 3)


def to_rows(tensor4):
    return tensor4.transpose(0, 2, 1, 3).reshape(-1, tensor4.shape[1] * tensor4.shape[3])


def block_scores(query_block, keys, offset, scale_att):
    scores = (
        jnp.einsum("shqe,shke->shqk", query_block, keys, preferred_element_type=jnp.float32)
        * scale_att
    )
    query_pos = offset + jnp.arange(query_block.shape[2])
    key_pos = jnp.arange(keys.shape[2])
    return jnp.where(key_pos[None, :] <= query_pos[:, None], scores, MASK_FILL)


def attend(query_rows, keys, value_rows, scale_att):
    length = query_rows.shape[2]
    block_len = min(512, length)
    outputs = []
    log_totals = []
    for offset in range(0, length, block_len):
        query_block = query_rows[:, :, offset : offset + block_len]
        scores = block_scores(query_block, keys, offset, scale_att)
        largest = jnp.max(scores, axis=-1, keepdims=True)
        exponent = jnp.exp(scores - largest)
        summed = jnp.sum(exponent, axis=-1, keepdims=True)
        attention = exponent / summed
        log_totals.append(largest + jnp.log(summed))
        outputs.append(
            jnp.einsum(
                "shqk,shke->shqe",
                attention.astype(jnp.bfloat16),
                value_rows,
                preferred_element_type=jnp.float32,
            )
        )
    return (jnp.concatenate(outputs, axis=2), log_totals)


def attend_back(query_rows, keys, value_rows, log_totals, grad_heads, scale_att):
    length = query_rows.shape[2]
    block_len = min(512, length)
    grad_blocks = []
    grad_keys = jnp.zeros(keys.shape, jnp.float32)
    grad_values = jnp.zeros(value_rows.shape, jnp.float32)
    for number, offset in enumerate(range(0, length, block_len)):
        query_block = query_rows[:, :, offset : offset + block_len]
        grad_block = grad_heads[:, :, offset : offset + block_len]
        scores = block_scores(query_block, keys, offset, scale_att)
        attention = jnp.exp(scores - log_totals[number])
        grad_attn = jnp.einsum(
            "shqe,shke->shqk", grad_block, value_rows, preferred_element_type=jnp.float32
        )
        row_inner = jnp.sum(grad_attn * attention, axis=-1, keepdims=True)
        grad_scores = (attention * (grad_attn - row_inner)).astype(jnp.bfloat16)
        grad_blocks.append(
            jnp.einsum("shqk,shke->shqe", grad_scores, keys, preferred_element_type=jnp.float32)
            * scale_att
        )
        grad_keys = (
            grad_keys
            + jnp.einsum(
                "shqk,shqe->shke", grad_scores, query_block, preferred_element_type=jnp.float32
            )
            * scale_att
        )
        grad_values = grad_values + jnp.einsum(
            "shqk,shqe->shke",
            attention.astype(jnp.bfloat16),
            grad_block,
            preferred_element_type=jnp.float32,
        )
    return (jnp.concatenate(grad_blocks, axis=2), grad_keys, grad_values)


def update_step(gradient_term, moment, weight_matrix, average, learning_rate):
    updated_moment = MOMENTUM_FACTOR * moment + gradient_term
    updated_weight = weight_matrix * (
        1.0 - learning_rate * WEIGHT_DECAY * ADAPTER_SCALE
    ) - learning_rate * (gradient_term + MOMENTUM_FACTOR * updated_moment)
    new_average = AVERAGE_KEEP * average + (1.0 - AVERAGE_KEEP) * updated_weight
    return (updated_moment, updated_weight, new_average)


def local(
    inputs,
    cotangent,
    groups,
    counts,
    vector_parameters,
    query_value_bias,
    hidden_bias,
    query_key_value_weight,
    attention_output_weight,
    hidden_weight,
    hidden_output_weight,
    adapter_down,
    adapter_up,
    momentum_down,
    momentum_up,
    average_down,
    average_up,
):
    seq_count, length, width_value = inputs.shape
    row_count = seq_count * length
    resid_in = inputs.reshape(row_count, width_value).astype(jnp.float32)
    first_norm_output = layer_norm(resid_in, vector_parameters[0], vector_parameters[1]).astype(
        jnp.bfloat16
    )
    local_width = query_key_value_weight.shape[2]
    column_start = lax.axis_index("tensor") * local_width
    down_reduced = adapter_down.astype(jnp.bfloat16)
    up_reduced = adapter_up.astype(jnp.bfloat16)
    up_local = lax.dynamic_slice_in_dim(up_reduced, column_start, local_width, 2)
    projected_rows = jnp.einsum(
        "rd,cde->cre", first_norm_output, query_key_value_weight, preferred_element_type=jnp.float32
    )
    adapter_input = jnp.einsum(
        "wo,qob->qwb", first_norm_output, down_reduced, preferred_element_type=jnp.float32
    ).astype(jnp.bfloat16)
    adapter_output = jnp.einsum(
        "iga,iaj->igj", adapter_input, up_local, preferred_element_type=jnp.float32
    )
    query_rows = (
        projected_rows[0] + query_value_bias[0] + ADAPTER_SCALE * adapter_output[0]
    ).astype(jnp.bfloat16)
    keys_low = projected_rows[1].astype(jnp.bfloat16)
    value_reduced = (
        projected_rows[2] + query_value_bias[1] + ADAPTER_SCALE * adapter_output[1]
    ).astype(jnp.bfloat16)
    scale_att = HEAD ** (-0.5)
    query_heads = to_heads(query_rows, seq_count, length)
    key_heads = to_heads(keys_low, seq_count, length)
    value_heads = to_heads(value_reduced, seq_count, length)
    heads_out, log_totals = attend(query_heads, key_heads, value_heads, scale_att)
    merged = to_rows(heads_out).astype(jnp.bfloat16)
    attn_part = jnp.dot(merged, attention_output_weight, preferred_element_type=jnp.float32)
    tile = row_count // lax.axis_size("tensor")
    row_offset = lax.axis_index("tensor") * tile
    one_hot = groups[:, None] == jnp.arange(counts.shape[0])[None, :]
    seq_counts = jnp.sum(jnp.where(one_hot, counts[None, :], 0), axis=1).astype(jnp.float32)
    seq_weight = COUNT_BASE / seq_counts
    grad_out = (cotangent.astype(jnp.float32) * seq_weight[:, None, None]).reshape(
        row_count, width_value
    )
    grad_low = grad_out.astype(jnp.bfloat16)
    attn_share = lax.psum_scatter(
        attn_part.astype(jnp.bfloat16), "tensor", scatter_dimension=0, tiled=True
    ).astype(jnp.float32)
    input_share = lax.dynamic_slice_in_dim(resid_in, row_offset, tile, 0)
    resid_share = input_share + attn_share + vector_parameters[4]
    norm_share = layer_norm(resid_share, vector_parameters[2], vector_parameters[3]).astype(
        jnp.bfloat16
    )
    norm2 = lax.all_gather(norm_share, "tensor", axis=0, tiled=True)
    preact = jnp.dot(norm2, hidden_weight, preferred_element_type=jnp.float32) + hidden_bias
    act_low = jax.nn.gelu(preact, approximate=True).astype(jnp.bfloat16)
    preact, mlp_part = (
        preact,
        jnp.dot(act_low, hidden_output_weight, preferred_element_type=jnp.float32),
    )
    mlp_share = lax.psum_scatter(
        mlp_part.astype(jnp.bfloat16), "tensor", scatter_dimension=0, tiled=True
    ).astype(jnp.float32)
    output_share = (resid_share + mlp_share + vector_parameters[5]).astype(jnp.bfloat16)
    output_rows = lax.all_gather(output_share, "tensor", axis=0, tiled=True)
    grad_act = jnp.einsum(
        "rd,fd->rf", grad_low, hidden_output_weight, preferred_element_type=jnp.float32
    )
    grad_pre = gelu_back(preact, grad_act).astype(jnp.bfloat16)
    grad_norm_share = lax.psum_scatter(
        jnp.einsum("rf,df->rd", grad_pre, hidden_weight, preferred_element_type=jnp.float32).astype(
            jnp.bfloat16
        ),
        "tensor",
        scatter_dimension=0,
        tiled=True,
    ).astype(jnp.float32)
    grad_out_share = lax.dynamic_slice_in_dim(grad_out, row_offset, tile, 0)
    grad_resid_share = grad_out_share + norm_back(
        resid_share, vector_parameters[2], vector_parameters[3], grad_norm_share
    )
    grad_resid_low = lax.all_gather(
        grad_resid_share.astype(jnp.bfloat16), "tensor", axis=0, tiled=True
    )
    grad_merged = jnp.einsum(
        "rd,ed->re", grad_resid_low, attention_output_weight, preferred_element_type=jnp.float32
    ).astype(jnp.bfloat16)
    grad_q, grad_k, grad_v = attend_back(
        query_heads,
        key_heads,
        value_heads,
        log_totals,
        to_heads(grad_merged, seq_count, length),
        scale_att,
    )
    grad_qkv = jnp.stack([to_rows(grad_q), to_rows(grad_k), to_rows(grad_v)]).astype(jnp.bfloat16)
    grad_norm1 = jnp.einsum(
        "cre,cde->rd", grad_qkv, query_key_value_weight, preferred_element_type=jnp.float32
    )
    query_value_gradient = jnp.stack([grad_qkv[0], grad_qkv[2]])
    adapter_input_gradient = ADAPTER_SCALE * jnp.einsum(
        "cre,cke->crk", query_value_gradient, up_local, preferred_element_type=jnp.float32
    )
    grad_norm1 = grad_norm1 + jnp.einsum(
        "ibp,inp->bn",
        adapter_input_gradient,
        down_reduced.astype(jnp.float32),
        precision=lax.Precision.HIGHEST,
    )
    grad_a_part = jnp.einsum(
        "rd,crk->cdk",
        first_norm_output,
        adapter_input_gradient,
        precision=lax.Precision.HIGHEST,
        preferred_element_type=jnp.float32,
    )
    local_up_gradient = ADAPTER_SCALE * jnp.einsum(
        "ipg,ipd->igd", adapter_input, query_value_gradient, preferred_element_type=jnp.float32
    )
    grad_b_part = lax.dynamic_update_slice(
        jnp.zeros((2, adapter_up.shape[1], width_value), jnp.float32),
        local_up_gradient,
        (0, 0, column_start),
    )
    grad_norm1_share = lax.psum_scatter(
        grad_norm1.astype(jnp.bfloat16), "tensor", scatter_dimension=0, tiled=True
    ).astype(jnp.float32)
    grad_input_share = grad_resid_share + norm_back(
        input_share, vector_parameters[0], vector_parameters[1], grad_norm1_share
    )
    grad_a_sum, grad_b_sum, weight_sum = lax.psum(
        (grad_a_part, grad_b_part, jnp.sum(seq_weight)), ("dp", "tensor")
    )
    mean_weight = weight_sum / (lax.axis_size("dp") * lax.axis_size("tensor") * seq_count)
    tokens_all = lax.axis_size("dp") * seq_count * length
    input_grad = lax.all_gather(
        (grad_input_share / mean_weight).astype(jnp.bfloat16), "tensor", axis=0, tiled=True
    )
    down_gradient = grad_a_sum / (mean_weight * tokens_all)
    up_gradient = grad_b_sum / (mean_weight * tokens_all)
    learning_rate = RATE_BASE * math.sqrt(tokens_all)
    updated_momentum_down, updated_down, updated_average_down = update_step(
        down_gradient, momentum_down, adapter_down, average_down, learning_rate
    )
    updated_momentum_up, updated_up, updated_average_up = update_step(
        up_gradient, momentum_up, adapter_up, average_up, learning_rate
    )
    block_out = output_rows.reshape(seq_count, length, width_value)
    input_grad = input_grad.reshape(seq_count, length, width_value)
    return (
        block_out,
        input_grad,
        down_gradient,
        up_gradient,
        updated_momentum_down,
        updated_momentum_up,
        updated_down,
        updated_up,
        updated_average_down,
        updated_average_up,
        updated_down.astype(jnp.bfloat16),
        updated_up.astype(jnp.bfloat16),
    )


QUARTER = 256
LANES = 128
BIAS_ROWS = 16
F32 = jnp.float32
BF16 = jnp.bfloat16
NT = (((1,), (1,)), ((), ()))


def dot(a, b):
    return lax.dot_general(a, b, (((1,), (0,)), ((), ())), preferred_element_type=F32)


def dot_nt(a, b):
    return lax.dot_general(a, b, NT, preferred_element_type=F32)


def parity(t):
    return (t ^ (t >> 1)) & 1


def tok_block(t):
    return parity(t) * 2 + ((t >> 1) & 1)


def rows_stats(rows):
    mean = jnp.mean(rows, axis=-1, keepdims=True)
    center = rows - mean
    rstd = lax.rsqrt(jnp.mean(center * center, axis=-1, keepdims=True) + NORM_EPS)
    return center * rstd, rstd


def norm_grad(xhat, rstd, gain, upstream):
    e = upstream * gain
    inner = jnp.mean(e * xhat, axis=-1, keepdims=True)
    return rstd * (e - jnp.mean(e, axis=-1, keepdims=True) - xhat * inner)


def seq_weight_of(groups_ref, counts_ref):
    count = counts_ref[groups_ref[0]]
    return COUNT_BASE / jnp.full((1, LANES), count, jnp.int32).astype(F32)


def cost(flops, nbytes, trans=0):
    return pl.CostEstimate(flops=int(flops), bytes_accessed=int(nbytes), transcendentals=int(trans))


def whole(shape):
    return pl.BlockSpec(shape, lambda *a: (0,) * len(shape))


def smem():
    return pl.BlockSpec(memory_space=pltpu.SMEM)


def call(
    kernel, grid, in_specs, out_specs, out_shape, args, prefetch, scratch=(), est=None, vmem=48
):
    return pl.pallas_call(
        kernel,
        grid_spec=pltpu.PrefetchScalarGridSpec(
            num_scalar_prefetch=len(prefetch),
            grid=grid,
            in_specs=in_specs,
            out_specs=out_specs,
            scratch_shapes=list(scratch),
        ),
        out_shape=out_shape,
        cost_estimate=est,
        compiler_params=pltpu.CompilerParams(vmem_limit_bytes=vmem * 1024 * 1024),
    )(*prefetch, *args)


def sds(shape, dtype):
    return jax.ShapeDtypeStruct(shape, dtype)


def fill_pack(out_ref, wh_ref, wo_ref, hb_ref):
    width = wh_ref.shape[0]
    out_ref[0, 0:width, :] = wh_ref[...]
    for j in range(width // QUARTER):
        out_ref[0, width + QUARTER * j : width + QUARTER * (j + 1), :] = wo_ref[
            :, QUARTER * j : QUARTER * (j + 1)
        ]
    bias = hb_ref[...]
    high = bias.astype(BF16)
    rest = bias - high.astype(F32)
    mid = rest.astype(BF16)
    low = (rest - mid.astype(F32)).astype(BF16)
    row = lax.broadcasted_iota(jnp.int32, (BIAS_ROWS, QUARTER), 0)
    spread = lambda v: jnp.broadcast_to(v.astype(F32), (BIAS_ROWS, QUARTER))
    packed = jnp.where(row == 0, spread(high), jnp.where(row == 1, spread(mid), spread(low)))
    out_ref[0, 2 * width : 2 * width + BIAS_ROWS, :] = jnp.where(row < 3, packed, 0.0).astype(BF16)


def pack_kernel(which_ref, wh_ref, wo_ref, hb_ref, out_ref):
    fill_pack(out_ref, wh_ref, wo_ref, hb_ref)


def fetch_kernel(core_ref, whx, wox, hbx, why, woy, hby, proj_ref, x_ref, y_ref, d_ref):
    width = whx.shape[0]
    half = proj_ref.shape[0]
    for ref, ops in ((x_ref, (whx, wox, hbx)), (y_ref, (why, woy, hby))):
        fill_pack(ref, *ops)
        for j in range(width // QUARTER):
            base = 2 * width + BIAS_ROWS + half * j
            ref[0, base : base + half, :] = proj_ref[:, QUARTER * j : QUARTER * (j + 1)]
    d_ref[...] = proj_ref[...]


def fetch_packs(core, hidden_weight, hidden_output_weight, hidden_bias, projection):
    width = hidden_weight.shape[0]
    half = projection.shape[0] // 2
    rows = 2 * width + BIAS_ROWS + half * (width // QUARTER)
    bias = hidden_bias.reshape(1, -1)
    triple = (hidden_weight, hidden_output_weight, bias)
    specs = []
    for base in (0, 2):
        specs += [
            pl.BlockSpec((width, QUARTER), lambda i, c, base=base: (0, base + c[0])),
            pl.BlockSpec((QUARTER, width), lambda i, c, base=base: (base + c[0], 0)),
            pl.BlockSpec((1, QUARTER), lambda i, c, base=base: (0, base + c[0])),
        ]
    return call(
        fetch_kernel,
        (1,),
        specs + [pl.BlockSpec((half, width), lambda i, c: (c[0], 0))],
        [whole((1, rows, QUARTER)), whole((1, rows, QUARTER)), whole((half, width))],
        [sds((1, rows, QUARTER), BF16)] * 2 + [sds((half, width), BF16)],
        (*triple, *triple, projection),
        (core,),
        est=cost(0, 8 * rows * QUARTER),
        vmem=62,
    )


def pack(which, count, hidden_weight, hidden_output_weight, hidden_bias):
    width = hidden_weight.shape[0]
    rows = 2 * width + BIAS_ROWS
    return call(
        pack_kernel,
        (count,),
        [
            pl.BlockSpec((width, QUARTER), lambda i, w: (0, w[i])),
            pl.BlockSpec((QUARTER, width), lambda i, w: (w[i], 0)),
            pl.BlockSpec((1, QUARTER), lambda i, w: (0, w[i])),
        ],
        pl.BlockSpec((1, rows, QUARTER), lambda i, w: (i, 0, 0)),
        sds((count, rows, QUARTER), BF16),
        (hidden_weight, hidden_output_weight, hidden_bias.reshape(1, -1)),
        (which,),
        est=cost(0, 4 * rows * QUARTER * count),
    )


def qkv_kernel(
    meta_ref, x_ref, vec_ref, w_ref, qvb_ref, down_ref, up_ref,
    q_ref, k_ref, v_ref, n_ref, lora_ref, down_s, up_s,
):
    rank = down_ref.shape[1]
    cols = w_ref.shape[2]

    @pl.when(pl.program_id(0) == 0)
    def _():
        down_s[...] = jnp.zeros_like(down_s)
        up_s[...] = jnp.zeros_like(up_s)
        down_s[0 : 2 * rank, :] = jnp.concatenate([down_ref[0], down_ref[1]], axis=0)
        up_s[0:rank, 0:cols] = up_ref[0]
        up_s[rank : 2 * rank, cols : 2 * cols] = up_ref[1]

    xhat, _ = rows_stats(x_ref[0].astype(F32))
    norm1 = (xhat * vec_ref[0:1, :] + vec_ref[1:2, :]).astype(BF16)
    n_ref[...] = norm1
    lora = dot_nt(norm1, down_s[...].astype(BF16)).astype(BF16)
    lora_ref[...] = lora
    adapt = ADAPTER_SCALE * dot(lora, up_s[...].astype(BF16))
    q = dot(norm1, w_ref[0]) + qvb_ref[0:1, :] + adapt[:, 0:cols]
    q_ref[...] = q.astype(BF16)
    k_ref[...] = dot(norm1, w_ref[1]).astype(BF16)
    v = dot(norm1, w_ref[2]) + qvb_ref[1:2, :] + adapt[:, cols : 2 * cols]
    v_ref[...] = v.astype(BF16)


def qkv(meta, x, vec, w, qvb, down_t, up):
    length, width = x.shape[1:]
    cols = w.shape[2]
    rank = up.shape[1]
    block = pl.BlockSpec((QUARTER, cols), lambda i, m: (i, 0))
    return call(
        qkv_kernel,
        (length // QUARTER,),
        [
            pl.BlockSpec((1, QUARTER, width), lambda i, m: (0, i, 0)),
            whole(vec.shape),
            whole(w.shape),
            whole(qvb.shape),
            whole(down_t.shape),
            pl.BlockSpec((2, rank, cols), lambda i, m: (0, 0, m[0] & 3)),
        ],
        [
            block,
            block,
            block,
            pl.BlockSpec((QUARTER, width), lambda i, m: (i, 0)),
            pl.BlockSpec((QUARTER, LANES), lambda i, m: (i, 0)),
        ],
        [
            sds((length, cols), BF16),
            sds((length, cols), BF16),
            sds((length, cols), BF16),
            sds((length, width), BF16),
            sds((length, LANES), BF16),
        ],
        (x, vec, w, qvb, down_t, up),
        (meta,),
        scratch=[pltpu.VMEM((LANES, width), F32), pltpu.VMEM((LANES, 2 * cols), F32)],
        est=cost(2 * length * width * 3 * cols, 4 * length * width + 6 * width * cols + 6 * length * cols),
    )


def head_lanes(value, head):
    lane = lax.broadcasted_iota(jnp.int32, value.shape, 1)
    return jnp.where(lane // HEAD == head, value, jnp.zeros_like(value))


def attend_kernel(meta_ref, q_ref, k_ref, v_ref, p_ref, ot_ref, same_ref, other_ref, vt_s, o_s):
    length = q_ref.shape[0]
    half = length // 2
    vt_s[...] = v_ref[...].astype(F32).T.astype(BF16)
    below = lax.broadcasted_iota(jnp.int32, (QUARTER, QUARTER), 0) <= lax.broadcasted_iota(
        jnp.int32, (QUARTER, QUARTER), 1
    )

    @pl.loop(0, 2)
    def _(head):
        rows = pl.ds(pl.multiple_of(head * HEAD, HEAD), HEAD)
        for j in range(length // QUARTER):
            at = slice(QUARTER * j, QUARTER * (j + 1))
            seen = QUARTER * (j + 1)
            query = head_lanes(q_ref[at, :], head) * jnp.asarray(HEAD ** (-0.5), BF16)
            scores = dot_nt(k_ref[0:seen, :], query)
            last = jnp.where(below, scores[QUARTER * j :, :], MASK_FILL)
            scores = last if j == 0 else jnp.concatenate([scores[: QUARTER * j, :], last], axis=0)
            top = jnp.max(scores, axis=0, keepdims=True)
            exponent = jnp.exp(scores - top)
            inverse = 1.0 / jnp.sum(exponent, axis=0, keepdims=True)
            probs = (exponent * inverse).astype(BF16)
            p_ref[head, 0:seen, at] = probs
            ot_ref[rows, at] = dot(vt_s[rows, 0:seen], probs)

    o_s[...] = ot_ref[...].T.astype(BF16)
    start = pl.multiple_of(parity(meta_ref[0] & 3) * half, half)
    same_ref[...] = o_s[pl.ds(start, half), :]
    other_ref[...] = o_s[pl.ds(pl.multiple_of(half - start, half), half), :]


def attend_fast(meta, q, k, v):
    length, cols = q.shape
    pairs = cols // LANES
    block = pl.BlockSpec((length, LANES), lambda g, m: (0, g))
    half = pl.BlockSpec((length // 2, LANES), lambda g, m: (0, g))
    return call(
        attend_kernel,
        (pairs,),
        [block, block, block],
        [
            pl.BlockSpec((2, length, length), lambda g, m: (g, 0, 0)),
            pl.BlockSpec((LANES, length), lambda g, m: (g, 0)),
            half,
            half,
        ],
        [
            sds((2 * pairs, length, length), BF16),
            sds((cols, length), F32),
            sds((length // 2, cols), BF16),
            sds((length // 2, cols), BF16),
        ],
        (q, k, v),
        (meta,),
        scratch=[pltpu.VMEM((LANES, length), BF16), pltpu.VMEM((length, LANES), BF16)],
        est=cost(8 * length * length * cols, 4 * length * length * pairs + 10 * length * cols),
    )


def attend_back_kernel(
    meta_ref, q_ref, k_ref, v_ref, p_ref, ot_ref, go_ref, gx_ref, gy_ref, gd_ref,
    dq_ref, dk_ref, dv_ref, g_s, gt_s, kt_s, dqt_s, dk_s, dv_s,
):
    length = q_ref.shape[0]
    t = meta_ref[0] & 3
    for piece, who in ((go_ref, t), (gx_ref, t ^ 1), (gy_ref, t ^ 2), (gd_ref, t ^ 3)):
        start = pl.multiple_of(tok_block(who) * QUARTER, QUARTER)
        g_s[pl.ds(start, QUARTER), :] = piece[...]
    gt_s[...] = g_s[...].astype(F32).T
    kt_s[...] = k_ref[...].astype(F32).T.astype(BF16)
    dk_s[...] = jnp.zeros_like(dk_s)
    dv_s[...] = jnp.zeros_like(dv_s)
    scale = jnp.asarray(HEAD ** (-0.5), BF16)

    @pl.loop(0, 2)
    def _(head):
        rows = pl.ds(pl.multiple_of(head * HEAD, HEAD), HEAD)
        for j in range(length // QUARTER):
            at = slice(QUARTER * j, QUARTER * (j + 1))
            seen = QUARTER * (j + 1)
            query = head_lanes(q_ref[at, :], head) * scale
            grad = head_lanes(g_s[at, :], head)
            inner = jnp.sum(gt_s[rows, at] * ot_ref[rows, at], axis=0, keepdims=True)
            probs = p_ref[head, 0:seen, at]
            grad_probs = dot_nt(v_ref[0:seen, :], grad)
            grad_scores = (probs.astype(F32) * (grad_probs - inner)).astype(BF16)
            dv_s[0:seen, :] += dot(probs, grad)
            dk_s[0:seen, :] += dot(grad_scores, query)
            dqt_s[rows, at] = dot(kt_s[rows, 0:seen], grad_scores)

    dq_ref[...] = (dqt_s[...].T * (HEAD ** (-0.5))).astype(BF16)
    dk_ref[...] = dk_s[...].astype(BF16)
    dv_ref[...] = dv_s[...].astype(BF16)


def attend_back_fast(meta, q, k, v, probs, out_t, pieces):
    length, cols = q.shape
    pairs = cols // LANES
    block = pl.BlockSpec((length, LANES), lambda g, m: (0, g))
    piece = pl.BlockSpec((QUARTER, LANES), lambda g, m: (0, g))
    return call(
        attend_back_kernel,
        (pairs,),
        [
            block,
            block,
            block,
            pl.BlockSpec((2, length, length), lambda g, m: (g, 0, 0)),
            pl.BlockSpec((LANES, length), lambda g, m: (g, 0)),
            piece,
            piece,
            piece,
            piece,
        ],
        [block, block, block],
        [sds((length, cols), BF16)] * 3,
        (q, k, v, probs, out_t, *pieces),
        (meta,),
        scratch=[
            pltpu.VMEM((length, LANES), BF16),
            pltpu.VMEM((LANES, length), F32),
            pltpu.VMEM((LANES, length), BF16),
            pltpu.VMEM((LANES, length), F32),
            pltpu.VMEM((length, LANES), F32),
            pltpu.VMEM((length, LANES), F32),
        ],
        est=cost(16 * length * length * cols, 4 * length * length * pairs + 16 * length * cols),
    )


def mlp_kernel(
    meta_ref, groups_ref, counts_ref, x_ref, cot_ref, vec_ref,
    ho_ref, hx_ref, hy_ref, hd_ref, wof_ref,
    own_ref, xa_ref, xb_ref, ya_ref, yb_ref,
    gn_ref, mlp_ref, resid_ref, n2_s, low_s, h_s, gn_s, mlp_s, buf, sem,
):
    width = x_ref.shape[2]
    blocks = own_ref.shape[0]
    total = blocks + 4
    extras = (xa_ref, xb_ref, ya_ref, yb_ref)
    depth = own_ref.shape[1]

    def fetch(i, slot):
        @pl.when(i < blocks)
        def _():
            pltpu.make_async_copy(own_ref.at[jnp.minimum(i, blocks - 1)], buf.at[slot], sem.at[slot]).start()

        for n, ref in enumerate(extras):
            @pl.when(i == blocks + n)
            def _(ref=ref):
                pltpu.make_async_copy(ref.at[0, 0:depth], buf.at[slot], sem.at[slot]).start()

    fetch(0, 0)
    local = ho_ref.shape[1]
    for n, ref in enumerate((ho_ref, hx_ref, hy_ref, hd_ref)):
        h_s[:, local * n : local * (n + 1)] = ref[...]
    resid = x_ref[0].astype(F32) + dot(h_s[...], wof_ref[...]) + vec_ref[4:5, :]
    resid_ref[...] = resid
    xhat, _ = rows_stats(resid)
    n2_s[...] = (xhat * vec_ref[2:3, :] + vec_ref[3:4, :]).astype(BF16)
    weight = seq_weight_of(groups_ref, counts_ref)[:, 0:1]
    low_s[...] = (cot_ref[0].astype(F32) * weight).astype(BF16)
    gn_s[...] = jnp.zeros_like(gn_s)
    mlp_s[...] = jnp.zeros_like(mlp_s)

    @pl.loop(0, total)
    def _(i):
        slot = i & 1
        pltpu.make_async_copy(own_ref.at[0], buf.at[slot], sem.at[slot]).wait()

        @pl.when(i + 1 < total)
        def _():
            fetch(i + 1, 1 - slot)

        wh = buf[slot, 0:width, :]
        tail = buf[slot, 2 * width : 2 * width + BIAS_ROWS, :].astype(F32)
        bias = tail[0:1, :] + tail[1:2, :] + tail[2:3, :]
        pre = dot(n2_s[...], wh) + bias
        grad_act = jnp.zeros_like(pre)
        for j in range(width // QUARTER):
            piece = buf[slot, width + QUARTER * j : width + QUARTER * (j + 1), :]
            grad_act = grad_act + dot_nt(low_s[:, QUARTER * j : QUARTER * (j + 1)], piece)
        root = math.sqrt(2.0 / math.pi)
        square = pre * pre
        turn = jnp.tanh(root * (pre + 0.044715 * (square * pre)))
        act = (0.5 * pre * (1.0 + turn)).astype(BF16)
        slope = 0.5 * (1.0 + turn) + 0.5 * pre * (1.0 - turn * turn) * (
            root * (1.0 + 3.0 * 0.044715 * square)
        )
        grad_pre = (grad_act * slope).astype(BF16)
        gn_s[...] += dot_nt(grad_pre, wh)
        for j in range(width // QUARTER):
            piece = buf[slot, width + QUARTER * j : width + QUARTER * (j + 1), :]
            mlp_s[:, QUARTER * j : QUARTER * (j + 1)] += dot(act, piece)

    gn_ref[...] = gn_s[...].astype(gn_ref.dtype)
    mlp_ref[...] = mlp_s[...].astype(mlp_ref.dtype)


def mlp_fast(final, meta, groups, counts, x, cot, vec, heads, wof, packs):
    width = x.shape[2]
    local = heads[0].shape[1]
    kind = F32 if final else BF16
    flip = 0 if final else 3
    rows = pl.BlockSpec((1, QUARTER, width), lambda i, m: (0, tok_block((m[0] & 3) ^ flip), 0))
    head = pl.BlockSpec((QUARTER, local), lambda i, m: ((((m[0] & 3) ^ flip) >> 1) & 1, 0))
    any_ = pl.BlockSpec(memory_space=pl.ANY)
    out = whole((QUARTER, width))
    depth = 2 * width + BIAS_ROWS
    hidden = QUARTER * (packs[0].shape[0] + 4)
    return call(
        mlp_kernel,
        (1,),
        [smem(), smem(), rows, rows, whole(vec.shape), head, head, head, head, whole(wof.shape)]
        + [any_] * 5,
        [out, out, out],
        [sds((QUARTER, width), kind), sds((QUARTER, width), kind), sds((QUARTER, width), F32)],
        (groups, counts, x, cot, vec, *heads, wof, *packs),
        (meta,),
        scratch=[
            pltpu.VMEM((QUARTER, width), BF16),
            pltpu.VMEM((QUARTER, width), BF16),
            pltpu.VMEM((QUARTER, 4 * local), BF16),
            pltpu.VMEM((QUARTER, width), F32),
            pltpu.VMEM((QUARTER, width), F32),
            pltpu.VMEM((2, depth, QUARTER), BF16),
            pltpu.SemaphoreType.DMA((2,)),
        ],
        est=cost(
            8 * QUARTER * width * hidden + 2 * QUARTER * width * width,
            4 * width * hidden + 2 * width * width + 16 * QUARTER * width,
            QUARTER * hidden,
        ),
    )


def project_kernel(meta_ref, own_ref, x0, x1, y0, y1, d0, d1, wof_ref):
    core = (meta_ref[0] >> 2) & 1
    local, width = own_ref.shape
    half = local // 2
    wof_ref[0:local, :] = own_ref[...]
    for n, (first, second) in enumerate(((x0, x1), (y0, y1), (d0, d1))):
        for ref, at in ((first, core), (second, 1 - core)):
            start = pl.multiple_of(local * (n + 1) + at * half, half)
            if n == 2:
                wof_ref[pl.ds(start, half), :] = ref[...]
            else:
                for j in range(width // QUARTER):
                    wof_ref[pl.ds(start, half), QUARTER * j : QUARTER * (j + 1)] = ref[
                        0, BIAS_ROWS + half * j : BIAS_ROWS + half * (j + 1), :
                    ]


def project(meta, own, packs, halves):
    local, width = own.shape
    depth = packs[0].shape[1]
    size = depth - 2 * width
    tail = pl.BlockSpec((pl.Element(1), pl.Element(size), pl.Element(QUARTER)), lambda i, m: (0, 2 * width, 0))
    return call(
        project_kernel,
        (1,),
        [whole(own.shape)] + [tail] * 4 + [whole(h.shape) for h in halves],
        whole((4 * local, width)),
        sds((4 * local, width), BF16),
        (own, *packs, *halves),
        (meta,),
        est=cost(0, 16 * local * width),
    )


def resid_back_kernel(
    meta_ref, groups_ref, counts_ref, own_ref, recv_ref, resid_ref, cot_ref, vec_ref, wof_ref,
    gr_ref, o_ref, x_ref, y_ref, d_ref,
):
    weight = seq_weight_of(groups_ref, counts_ref)[:, 0:1]
    grad = own_ref[...] + recv_ref[...].astype(F32)
    xhat, rstd = rows_stats(resid_ref[...])
    total = cot_ref[0].astype(F32) * weight + norm_grad(xhat, rstd, vec_ref[2:3, :], grad)
    gr_ref[...] = total
    low = total.astype(BF16)
    local = wof_ref.shape[0] // 4
    for n, ref in enumerate((o_ref, x_ref, y_ref, d_ref)):
        ref[...] = dot_nt(low, wof_ref[local * n : local * (n + 1), :]).astype(BF16)


def resid_back(meta, groups, counts, own, recv, resid, cot, vec, wof):
    width = own.shape[1]
    local = wof.shape[0] // 4
    piece = whole((QUARTER, local))
    full = whole((QUARTER, width))
    return call(
        resid_back_kernel,
        (1,),
        [
            smem(),
            smem(),
            full,
            full,
            full,
            pl.BlockSpec((1, QUARTER, width), lambda i, m: (0, tok_block(m[0] & 3), 0)),
            whole(vec.shape),
            whole(wof.shape),
        ],
        [full, piece, piece, piece, piece],
        [sds((QUARTER, width), F32)] + [sds((QUARTER, local), BF16)] * 4,
        (groups, counts, own, recv, resid, cot, vec, wof),
        (meta,),
        est=cost(2 * QUARTER * width * width, 16 * QUARTER * width + 2 * width * width),
    )


def adapter_inner(dq, dv, up_s, cols):
    ups = up_s[...].astype(BF16)
    return ADAPTER_SCALE * (dot_nt(dq, ups[:, 0:cols]) + dot_nt(dv, ups[:, cols : 2 * cols]))


def fill_up(up_s, up_ref, cols):
    rank = up_ref.shape[1]
    up_s[...] = jnp.zeros_like(up_s)
    for copy in (0, 2):
        up_s[copy * rank : (copy + 1) * rank, 0:cols] = up_ref[0]
        up_s[(copy + 1) * rank : (copy + 2) * rank, cols : 2 * cols] = up_ref[1]


def split_inner(inner, rank):
    high = inner.astype(BF16)
    low = (inner - high.astype(F32)).astype(BF16)
    lane = lax.broadcasted_iota(jnp.int32, inner.shape, 1)
    return jnp.where(lane < 2 * rank, high.astype(F32), low.astype(F32))


def grads_kernel(
    meta_ref, groups_ref, counts_ref, dq_ref, dv_ref, up_ref, n_ref, lora_ref,
    grads_ref, up_s, dn_s, gu_s,
):
    i = pl.program_id(0)
    rank = up_ref.shape[1]
    cols = dq_ref.shape[1]

    @pl.when(i == 0)
    def _():
        fill_up(up_s, up_ref, cols)
        dn_s[...] = jnp.zeros_like(dn_s)
        gu_s[...] = jnp.zeros_like(gu_s)

    dq, dv = dq_ref[...], dv_ref[...]
    split = split_inner(adapter_inner(dq, dv, up_s, cols), rank)
    dn_s[...] += dot(split.T.astype(BF16), n_ref[...])
    lt = lora_ref[...].astype(F32).T.astype(BF16)
    gu_s[...] += ADAPTER_SCALE * dot(lt, jnp.concatenate([dq, dv], axis=1))

    @pl.when(i == pl.num_programs(0) - 1)
    def _():
        grads_ref[...] = jnp.zeros_like(grads_ref)
        grads_ref[0 : 2 * rank, :] = dn_s[0 : 2 * rank, :] + dn_s[2 * rank : 4 * rank, :]
        start = pl.multiple_of((meta_ref[0] & 3) * cols, cols)
        grads_ref[2 * rank : 3 * rank, pl.ds(start, cols)] = gu_s[0:rank, 0:cols]
        grads_ref[3 * rank : 4 * rank, pl.ds(start, cols)] = gu_s[rank : 2 * rank, cols : 2 * cols]
        weight = seq_weight_of(groups_ref, counts_ref)[:, 0:1]
        grads_ref[4 * rank : 4 * rank + 8, :] = jnp.broadcast_to(weight, (8, grads_ref.shape[1]))


def adapter_grads(meta, groups, counts, dq, dv, up, norm1, lora):
    length, cols = dq.shape
    width = norm1.shape[1]
    rank = up.shape[1]
    rows = 2 * QUARTER
    block = pl.BlockSpec((rows, cols), lambda i, m: (i, 0))
    lanes = pl.BlockSpec((rows, LANES), lambda i, m: (i, 0))
    return call(
        grads_kernel,
        (length // rows,),
        [
            smem(),
            smem(),
            block,
            block,
            pl.BlockSpec((2, rank, cols), lambda i, m: (0, 0, m[0] & 3)),
            pl.BlockSpec((rows, width), lambda i, m: (i, 0)),
            lanes,
        ],
        whole((4 * rank + 8, width)),
        sds((4 * rank + 8, width), F32),
        (groups, counts, dq, dv, up, norm1, lora),
        (meta,),
        scratch=[
            pltpu.VMEM((LANES, 2 * cols), F32),
            pltpu.VMEM((LANES, width), F32),
            pltpu.VMEM((LANES, 2 * cols), F32),
        ],
        est=cost(2 * length * width * LANES, 2 * length * width + 4 * length * cols),
    )


def input_back_kernel(
    meta_ref, dq_ref, dk_ref, dv_ref, w_ref, down_ref, up_ref,
    ox_ref, oy_ref, od_ref, own_ref, down_s, up_s,
):
    i = pl.program_id(0)
    rank = down_ref.shape[1]
    cols = dq_ref.shape[1]

    @pl.when(i == 0)
    def _():
        fill_up(up_s, up_ref, cols)
        down_s[...] = jnp.zeros_like(down_s)
        both = jnp.concatenate([down_ref[0], down_ref[1]], axis=0)
        down_s[0 : 2 * rank, :] = both
        down_s[2 * rank : 4 * rank, :] = both

    dq, dv = dq_ref[...], dv_ref[...]
    split = split_inner(adapter_inner(dq, dv, up_s, cols), rank)
    grad = (
        dot_nt(dq, w_ref[0])
        + dot_nt(dk_ref[...], w_ref[1])
        + dot_nt(dv, w_ref[2])
        + dot(split.astype(BF16), down_s[...].astype(BF16))
    )
    for n, ref in enumerate((ox_ref, oy_ref, od_ref, own_ref)):
        @pl.when(i == n)
        def _(ref=ref):
            ref[...] = grad.astype(ref.dtype)


def input_back(meta, dq, dk, dv, w, down_t, up):
    length, cols = dq.shape
    width = w.shape[1]
    rank = up.shape[1]

    def who(i, m):
        return tok_block((m[0] & 3) ^ jnp.where(i == 3, 0, i + 1))

    block = pl.BlockSpec((QUARTER, cols), lambda i, m: (who(i, m), 0))
    out = whole((QUARTER, width))
    return call(
        input_back_kernel,
        (4,),
        [
            block,
            block,
            block,
            whole(w.shape),
            whole(down_t.shape),
            pl.BlockSpec((2, rank, cols), lambda i, m: (0, 0, m[0] & 3)),
        ],
        [out, out, out, out],
        [sds((QUARTER, width), BF16)] * 3 + [sds((QUARTER, width), F32)],
        (dq, dk, dv, w, down_t, up),
        (meta,),
        scratch=[pltpu.VMEM((LANES, width), F32), pltpu.VMEM((LANES, 2 * cols), F32)],
        est=cost(6 * length * width * cols, 6 * width * cols + 6 * length * cols + 6 * length * width),
    )


def first_back_kernel(meta_ref, own_ref, a_ref, b_ref, c_ref, x_ref, gr_ref, vec_ref, out_ref):
    grad = own_ref[...] + a_ref[...].astype(F32) + b_ref[...].astype(F32) + c_ref[...].astype(F32)
    xhat, rstd = rows_stats(x_ref[0].astype(F32))
    out_ref[...] = (gr_ref[...] + norm_grad(xhat, rstd, vec_ref[0:1, :], grad)).astype(BF16)


def first_back(meta, own, pieces, x, grad_resid, vec):
    width = own.shape[1]
    full = whole((QUARTER, width))
    return call(
        first_back_kernel,
        (1,),
        [
            full,
            full,
            full,
            full,
            pl.BlockSpec((1, QUARTER, width), lambda i, m: (0, tok_block(m[0] & 3), 0)),
            full,
            whole(vec.shape),
        ],
        full,
        sds((QUARTER, width), BF16),
        (own, *pieces, x, grad_resid, vec),
        (meta,),
        est=cost(30 * QUARTER * width, 16 * QUARTER * width),
    )


def gather_kernel(scaled, meta_ref, *refs):
    out_ref = refs[-1]
    pieces = refs[:-1]
    if scaled:
        factor = scaled / refs[0][0:1, 0:1]
        pieces = refs[1:-1]
    i = pl.program_id(0)
    for n in range(4):
        parts = pieces[3:] if n == 3 else pieces[n : n + 1]

        @pl.when(i == n)
        def _(parts=parts):
            start = 0
            for ref in parts:
                rows = ref.shape[0]
                value = ref[...]
                if scaled:
                    value = (value.astype(F32) * factor).astype(BF16)
                out_ref[0, start : start + rows, :] = value
                start += rows


def gather_rows(meta, pieces, scaled=0.0, total=None):
    width = pieces[0].shape[1]
    extra = [total] if scaled else []
    specs = [pl.BlockSpec((8, width), lambda i, m: (total.shape[0] // 8 - 1, 0))] if scaled else []
    return call(
        functools.partial(gather_kernel, scaled),
        (4,),
        specs + [whole(p.shape) for p in pieces],
        pl.BlockSpec((1, QUARTER, width), lambda i, m: (0, tok_block((m[0] & 3) ^ i), 0)),
        sds((1, 4 * QUARTER, width), BF16),
        (*extra, *pieces),
        (meta,),
        est=cost(0, 16 * QUARTER * width),
    )


def update_kernel(tokens, devices, total_ref, d_ref, u_ref, md_ref, mu_ref, ad_ref, au_ref, *outs):
    gd_o, gu_o, md_o, mu_o, d_o, u_o, ad_o, au_o, cd_o, cu_o = outs
    rank = d_ref.shape[1]
    weight = total_ref[4 * rank : 4 * rank + 1, 0:1]
    mean_weight = weight / devices
    rate = RATE_BASE * math.sqrt(tokens)
    for c in range(2):
        for base, g_o, m_ref, m_o, w_ref, w_o, a_ref, a_o, c_o in (
            (0, gd_o, md_ref, md_o, d_ref, d_o, ad_ref, ad_o, cd_o),
            (2 * rank, gu_o, mu_ref, mu_o, u_ref, u_o, au_ref, au_o, cu_o),
        ):
            gradient = total_ref[base + c * rank : base + (c + 1) * rank, :] / (mean_weight * tokens)
            moment, new, average = update_step(gradient, m_ref[c], w_ref[c], a_ref[c], rate)
            g_o[c] = gradient
            m_o[c] = moment
            w_o[c] = new
            a_o[c] = average
            c_o[c] = new.astype(BF16)


def update(tokens, devices, total, down_t, up, mom_d, mom_u, avg_d, avg_u):
    shapes = [whole(total.shape)] + [whole(down_t.shape)] * 6
    kinds = [F32] * 8 + [BF16] * 2
    return call(
        functools.partial(update_kernel, float(tokens), float(devices)),
        (1,),
        shapes,
        [whole(down_t.shape)] * 10,
        [sds(down_t.shape, kind) for kind in kinds],
        (total, down_t, up, mom_d, mom_u, avg_d, avg_u),
        (),
        est=cost(0, 18 * 4 * down_t.size),
    )


def local_fast(
    dp_size,
    inputs,
    cotangent,
    groups,
    counts,
    vector_parameters,
    query_value_bias,
    hidden_bias,
    query_key_value_weight,
    attention_output_weight,
    hidden_weight,
    hidden_output_weight,
    adapter_down,
    adapter_up,
    momentum_down,
    momentum_up,
    average_down,
    average_up,
):
    axes = ("dp", "tensor")

    def send(value, dp_flip, t_flip):
        pairs = [
            (d * 4 + t, (d ^ dp_flip) * 4 + (t ^ t_flip)) for d in range(dp_size) for t in range(4)
        ]
        return lax.ppermute(value, axes, pairs)

    tensor_at = lax.axis_index("tensor")
    core = lax.axis_index("dp") & 1
    meta = (tensor_at + 4 * core).astype(jnp.int32).reshape(1)
    down_t = jnp.swapaxes(adapter_down, 1, 2)
    vec = vector_parameters
    length = inputs.shape[1]

    one = core.astype(jnp.int32).reshape(1)
    ffn = (hidden_weight, hidden_output_weight, hidden_bias)
    pack_x, pack_y, pack_d = fetch_packs(one, *ffn, attention_output_weight)
    got_x = send(pack_x, 0, 1)
    got_y = send(pack_y, 0, 2)
    got_d = send(pack_d, 0, 3)

    q, k, v, norm1, lora = qkv(
        meta, inputs, vec, query_key_value_weight, query_value_bias, down_t, adapter_up
    )
    probs, out_t, same, other = attend_fast(meta, q, k, v)
    heads = [same, send(other, 0, 1), send(other, 0, 2), send(same, 0, 3)]
    swap_x = send(got_x, 1, 0)
    swap_y = send(got_y, 1, 0)
    swap_d = send(got_d, 1, 0)
    own_packs = pack(jnp.arange(4, dtype=jnp.int32), 4, *ffn)
    wof = project(
        meta, attention_output_weight, (got_x, swap_x, got_y, swap_y), (got_d, swap_d)
    )
    packs = [own_packs, got_x, swap_x, got_y, swap_y]

    gn_pair, mlp_pair, _ = mlp_fast(
        False, meta, groups, counts, inputs, cotangent, vec, heads, wof, packs
    )
    gn_recv = send(gn_pair, 0, 3)
    mlp_recv = send(mlp_pair, 0, 3)
    gn_own, mlp_own, resid = mlp_fast(
        True, meta, groups, counts, inputs, cotangent, vec, heads, wof, packs
    )
    grad_resid, g_own, g_x, g_y, g_d = resid_back(
        meta, groups, counts, gn_own, gn_recv, resid, cotangent, vec, wof
    )
    pieces = [g_own, send(g_x, 0, 1), send(g_y, 0, 2), send(g_d, 0, 3)]
    out_own = (resid + mlp_own + mlp_recv.astype(F32) + vec[5]).astype(BF16)
    half = QUARTER // 2

    def spread(own):
        from_x = send(own, 0, 1)
        from_y = send(own, 0, 2)
        cut_x, cut_y = from_x[:half], from_y[half:]
        return [own, from_x, from_y, send(cut_x, 0, 2), send(cut_y, 0, 1)]

    out_all = spread(out_own)

    dq, dk, dv = attend_back_fast(meta, q, k, v, probs, out_t, pieces)
    gx, gy, gd, g1_own = input_back(
        meta, dq, dk, dv, query_key_value_weight, down_t, adapter_up
    )
    g1 = [send(gx, 0, 1), send(gy, 0, 2), send(gd, 0, 3)]
    total = adapter_grads(meta, groups, counts, dq, dv, adapter_up, norm1, lora)
    sum_x = send(total, 0, 1)
    sum_y = send(total, 0, 2)
    sum_d = send(total, 0, 3)
    total = (total + sum_x) + (sum_y + sum_d)
    step = 1
    while step < dp_size:
        got = send(total, step, 0)
        total = total + got
        step *= 2
    in_own = first_back(meta, g1_own, g1, inputs, grad_resid, vec)
    in_all = spread(in_own)
    block_out = gather_rows(meta, out_all)
    copies = dp_size * 4
    input_grad = gather_rows(meta, in_all, scaled=float(copies), total=total)
    results = update(
        dp_size * length,
        copies,
        total,
        down_t,
        adapter_up,
        jnp.swapaxes(momentum_down, 1, 2),
        momentum_up,
        jnp.swapaxes(average_down, 1, 2),
        average_up,
    )
    results = [
        jnp.swapaxes(value, 1, 2) if number % 2 == 0 else value
        for number, value in enumerate(results)
    ]
    return (block_out, input_grad, *results)


def solution(mesh):
    in_specs = (
        P("dp", None, None),
        P("dp", None, None),
        P("dp"),
        P(),
        P(),
        P(None, "tensor"),
        P("tensor"),
        P(None, None, "tensor"),
        P("tensor", None),
        P(None, "tensor"),
        P("tensor", None),
        P(),
        P(),
        P(),
        P(),
        P(),
        P(),
    )
    out_specs = (
        P("dp", None, None),
        P("dp", None, None),
        P(),
        P(),
        P(),
        P(),
        P(),
        P(),
        P(),
        P(),
        P(),
        P(),
    )
    dp_size = mesh.shape["dp"]
    small = mesh.shape["tensor"] == 4 and dp_size & (dp_size - 1) == 0 and dp_size > 1

    def body(*args):
        if small and args[0].shape[0] == 1 and args[0].shape[1] == 4 * QUARTER:
            return local_fast(dp_size, *args)
        return local(*args)

    return jax.shard_map(body, mesh=mesh, in_specs=in_specs, out_specs=out_specs, check_vma=False)
```

profile of v0, /device:TPU:0, one launch (start us, length us, event | category | flops | bytes accessed | tf_op | source)
XLA Modules:
  0.0 211.4 jit_solution(10824012115902021054)
XLA Ops:
  0.7 3.3 %shard_map.258 = (bf16[1,2576,256]{2,1,0:T(8,128)(2,1)}, bf16[1,2576,256]{2,1,0:T(8,128)(2,1)}, bf16[128,1024]{1,0:T(8,128)(2,1)}) custom-call(s32[1]{0:T(128)} %bitcast.2.core_ref, bf16[1024,1024]{1,0:T(8,128)(2,1)} %wh_ref.1, bf16[1024,1024]{1,0:T(8,128)(2,1)} %wo_ref.1, f32[1,1024]{1,0:T(1,128)} %bitcast.12, bf16[1024,1024]{1,0:T(8,128)(2,1)} %wh_ref.1, ...), custom_call_target="tpu_custom_call" | custom-call | bytes 5275648 | tf_op jit(solution)/shard_map/pallas_call | solution.py:375
  4.0 3.0 %collective-permute-start.3 = (bf16[1,2576,256]{2,1,0:T(8,128)(2,1)}, bf16[1,2576,256]{2,1,0:T(8,128)(2,1)S(1)}, u32[]{:S(2)}, u32[]{:S(2)}) collective-permute-start(bf16[1,2576,256]{2,1,0:T(8,128)(2,1)} %get-tuple-element.56), channel_id=1, source_target_pairs={{0,1},{1,0},{2,3},{3,2},{4,5},{5,4},{6,7},{7,6},{8,9},{9,8},{10,11... | collective-permute-start | bytes 3956744 | tf_op jit(solution)/shard_map/ppermute | solution.py:1124
  7.0 1.5 collective-permute-start.5
  8.5 27.6 %collective-permute-done.3.x0.xa_ref = bf16[1,2576,256]{2,1,0:T(8,128)(2,1)S(1)} collective-permute-done((bf16[1,2576,256]{2,1,0:T(8,128)(2,1)}, bf16[1,2576,256]{2,1,0:T(8,128)(2,1)S(1)}, u32[]{:S(2)}, u32[]{:S(2)}) %collective-permute-start.3) | collective-permute-done | bytes 1318944 | tf_op jit(solution)/shard_map/ppermute | solution.py:1124
  36.2 1.5 collective-permute-done.5.y0.ya_ref
  37.6 1.7 collective-permute-start.7
  39.4 8.1 %collective-permute-done.7.d0 = bf16[128,1024]{1,0:T(8,128)(2,1)S(1)} collective-permute-done((bf16[128,1024]{1,0:T(8,128)(2,1)}, bf16[128,1024]{1,0:T(8,128)(2,1)S(1)}, u32[]{:S(2)}, u32[]{:S(2)}) %collective-permute-start.7) | collective-permute-done | bytes 262176 | tf_op jit(solution)/shard_map/ppermute | solution.py:1124
  47.5 1.4 copy-done.13
  48.9 6.6 %shard_map.256 = (bf16[1024,256]{1,0:T(8,128)(2,1)S(1)}, bf16[1024,256]{1,0:T(8,128)(2,1)S(1)}, bf16[1024,256]{1,0:T(8,128)(2,1)S(1)}, bf16[1024,1024]{1,0:T(8,128)(2,1)S(1)}, bf16[1024,128]{1,0:T(8,128)(2,1)S(1)}) custom-call(s32[1]{0:T(128)} %bitcast.meta_ref, bf16[1,1024,1024]{2,1,0:T(8,128)(2,1)} %x_ref.7, f32[6,1024]{1,0:T(8,128)S(1)} %copy-done.4, ...), custom_call_target="tpu_custom_call" | custom-call | flops 1610612736 | bytes 7340032 | tf_op jit(solution)/shard_map/pallas_call | solution.py:375
  55.5 0.0 copy-start
  55.5 12.5 %shard_map.257 = (bf16[4,1024,1024]{2,1,0:T(8,128)(2,1)}, f32[256,1024]{1,0:T(8,128)S(1)}, bf16[512,256]{1,0:T(8,128)(2,1)S(1)}, bf16[512,256]{1,0:T(8,128)(2,1)S(1)}) custom-call(s32[1]{0:T(128)} %bitcast.meta_ref, bf16[1024,256]{1,0:T(8,128)(2,1)S(1)} %get-tuple-element.51.q_ref, bf16[1024,256]{1,0:T(8,128)(2,1)S(1)} %get-tuple-element.52.k_ref, ...), custom_call_target="tpu_custom_call" | custom-call | flops 2147483648 | bytes 11010048 | tf_op jit(solution)/shard_map/pallas_call | solution.py:375
  68.0 0.4 collective-permute-start
  68.3 1.7 collective-permute-start.1
  70.0 1.4 collective-permute-start.2
  72.2 0.0 copy-start.2
  72.2 3.4 %shard_map.260.own_ref = bf16[4,2064,256]{2,1,0:T(8,128)(2,1)} custom-call(s32[4]{0:T(128)S(1)} %iota.3.which_ref, bf16[1024,1024]{1,0:T(8,128)(2,1)S(1)} %copy-done, bf16[1024,1024]{1,0:T(8,128)(2,1)S(1)} %copy-done.1, f32[1,1024]{1,0:T(1,128)S(1)} %bitcast.14), custom_call_target="tpu_custom_call" | custom-call | bytes 8454144 | tf_op jit(solution)/shard_map/pallas_call | solution.py:375
  75.6 2.5 %shard_map.259.wof_ref = bf16[1024,1024]{1,0:T(8,128)(2,1)} custom-call(s32[1]{0:T(128)} %bitcast.meta_ref, bf16[256,1024]{1,0:T(8,128)(2,1)S(1)} %copy-done.2, bf16[1,2576,256]{2,1,0:T(8,128)(2,1)S(1)} %collective-permute-done.3.x0.xa_ref, bf16[1,2576,256]{2,1,0:T(8,128)(2,1)} %collective-permute-done.4.x1.xb_ref, ...), custom_call_target="tpu_custom_call" | custom-call | bytes 4194304 | tf_op jit(solution)/shard_map/pallas_call | solution.py:375
  78.1 3.5 %collective-permute-done.1.hy_ref = bf16[512,256]{1,0:T(8,128)(2,1)S(1)} collective-permute-done((bf16[512,256]{1,0:T(8,128)(2,1)S(1)}, bf16[512,256]{1,0:T(8,128)(2,1)S(1)}, u32[]{:S(2)}, u32[]{:S(2)}) %collective-permute-start.1) | collective-permute-done | bytes 262176 | tf_op jit(solution)/shard_map/ppermute | solution.py:1124
  81.6 1.6 collective-permute-done.2.hd_ref
  83.3 13.4 %shard_map.262 = (bf16[256,1024]{1,0:T(8,128)(2,1)S(1)}, bf16[256,1024]{1,0:T(8,128)(2,1)S(1)}, f32[256,1024]{1,0:T(8,128)}) custom-call(s32[1]{0:T(128)} %bitcast.meta_ref, s32[1]{0:T(128)S(6)} %copy.29.groups_ref, s32[8]{0:T(128)S(1)} %copy-done.12, bf16[1,1024,1024]{2,1,0:T(8,128)(2,1)} %x_ref.7, bf16[1,1024,1024]{2,1,0:T(8,128)(2,1)} %cot_ref.5, ...), custom_call_target="tpu_custom_call" | custom-call | flops 4831838208 | bytes 14680064 | tf_op jit(solution)/shard_map/pallas_call | solution.py:375
  96.7 1.8 collective-permute-start.14
  98.5 13.4 %shard_map.261 = (f32[256,1024]{1,0:T(8,128)S(1)}, f32[256,1024]{1,0:T(8,128)S(1)}, f32[256,1024]{1,0:T(8,128)S(1)}) custom-call(s32[1]{0:T(128)} %bitcast.meta_ref, s32[1]{0:T(128)S(6)} %copy.29.groups_ref, s32[8]{0:T(128)S(1)} %copy-done.12, bf16[1,1024,1024]{2,1,0:T(8,128)(2,1)} %x_ref.7, bf16[1,1024,1024]{2,1,0:T(8,128)(2,1)} %cot_ref.5, ...), custom_call_target="tpu_custom_call" | custom-call | flops 4831838208 | bytes 14680064 | tf_op jit(solution)/shard_map/pallas_call | solution.py:375
  112.0 3.2 %shard_map.264 = (f32[256,1024]{1,0:T(8,128)S(1)}, bf16[256,256]{1,0:T(8,128)(2,1)S(1)}, bf16[256,256]{1,0:T(8,128)(2,1)S(1)}, bf16[256,256]{1,0:T(8,128)(2,1)S(1)}, bf16[256,256]{1,0:T(8,128)(2,1)S(1)}) custom-call(s32[1]{0:T(128)} %bitcast.meta_ref, s32[1]{0:T(128)S(6)} %copy.29.groups_ref, s32[8]{0:T(128)S(1)} %copy-done.12, ...), custom_call_target="tpu_custom_call" | custom-call | flops 536870912 | bytes 6291456 | tf_op jit(solution)/shard_map/pallas_call | solution.py:375
  115.2 0.6 collective-permute-start.15
  115.8 1.2 collective-permute-start.16
  117.0 1.8 collective-permute-start.17
  118.8 1.2 collective-permute-start.9
  120.0 1.7 collective-permute-done.15.gx_ref
  121.7 13.1 %collective-permute-done.16.gy_ref = bf16[256,256]{1,0:T(8,128)(2,1)S(1)} collective-permute-done((bf16[256,256]{1,0:T(8,128)(2,1)S(1)}, bf16[256,256]{1,0:T(8,128)(2,1)S(1)}, u32[]{:S(2)}, u32[]{:S(2)}) %collective-permute-start.16) | collective-permute-done | bytes 131104 | tf_op jit(solution)/shard_map/ppermute | solution.py:1124
  134.8 0.0 copy-start.14
  134.8 10.4 %shard_map.265 = (bf16[1024,256]{1,0:T(8,128)(2,1)S(1)}, bf16[1024,256]{1,0:T(8,128)(2,1)S(1)}, bf16[1024,256]{1,0:T(8,128)(2,1)S(1)}) custom-call(s32[1]{0:T(128)} %bitcast.meta_ref, bf16[1024,256]{1,0:T(8,128)(2,1)S(1)} %get-tuple-element.51.q_ref, bf16[1024,256]{1,0:T(8,128)(2,1)S(1)} %get-tuple-element.52.k_ref, bf16[1024,256]{1,0:T(8,128)(2,1)S(1)} %copy-done.17, ...), custom_call_target="tpu_custom_call" | custom-call | flops 4294967296 | bytes 12582912 | tf_op jit(solution)/shard_map/pallas_call | solution.py:375
  145.2 3.8 %shard_map.267 = (bf16[256,1024]{1,0:T(8,128)(2,1)S(1)}, bf16[256,1024]{1,0:T(8,128)(2,1)S(1)}, bf16[256,1024]{1,0:T(8,128)(2,1)S(1)}, f32[256,1024]{1,0:T(8,128)S(1)}) custom-call(s32[1]{0:T(128)} %bitcast.meta_ref, bf16[1024,256]{1,0:T(8,128)(2,1)S(1)} %get-tuple-element.70.dq_ref, bf16[1024,256]{1,0:T(8,128)(2,1)S(1)} %get-tuple-element.74.dk_ref, ...), custom_call_target="tpu_custom_call" | custom-call | flops 1610612736 | bytes 9437184 | tf_op jit(solution)/shard_map/pallas_call | solution.py:375
  149.0 1.0 collective-permute-start.24
  150.1 1.1 collective-permute-start.25
  151.2 1.4 collective-permute-start.26
  152.6 2.5 %shard_map.266 = f32[24,1024]{1,0:T(8,128)S(1)} custom-call(s32[1]{0:T(128)} %bitcast.meta_ref, s32[1]{0:T(128)S(6)} %copy.29.groups_ref, s32[8]{0:T(128)S(1)} %copy-done.12, bf16[1024,256]{1,0:T(8,128)(2,1)S(1)} %get-tuple-element.70.dq_ref, bf16[1024,256]{1,0:T(8,128)(2,1)S(1)} %get-tuple-element.71.dv_ref, f32[2,4,1024]{2,1,0:T(4,128)S(1)} %copy-done.5, ...), custom_call_target="tpu_custom_call" | custom-call | flops 268435456 | bytes 3145728 | tf_op jit(solution)/shard_map/pallas_call | solution.py:375
  155.1 0.8 collective-permute-start.19
  155.9 0.3 add_convert_fusion.refs_0_
  156.2 1.4 collective-permute-start.10
  157.6 6.3 %collective-permute-done.24.a_ref = bf16[256,1024]{1,0:T(8,128)(2,1)S(1)} collective-permute-done((bf16[256,1024]{1,0:T(8,128)(2,1)S(1)}, bf16[256,1024]{1,0:T(8,128)(2,1)S(1)}, u32[]{:S(2)}, u32[]{:S(2)}) %collective-permute-start.24) | collective-permute-done | bytes 524320 | tf_op jit(solution)/shard_map/ppermute | solution.py:1124
  163.9 0.8 collective-permute-start.11
  164.7 1.0 collective-permute-done.25.b_ref
  165.6 7.6 %collective-permute-done.26.c_ref = bf16[256,1024]{1,0:T(8,128)(2,1)S(1)} collective-permute-done((bf16[256,1024]{1,0:T(8,128)(2,1)S(1)}, bf16[256,1024]{1,0:T(8,128)(2,1)S(1)}, u32[]{:S(2)}, u32[]{:S(2)}) %collective-permute-start.26) | collective-permute-done | bytes 524320 | tf_op jit(solution)/shard_map/ppermute | solution.py:1124
  173.3 1.9 shard_map.268.refs_1_
  175.2 0.0 copy-start.10
  175.2 0.0 copy-start.11
  175.2 1.6 collective-permute-start.27
  176.9 0.8 collective-permute-start.28
  177.7 1.1 collective-permute-start.20
  178.8 8.1 %collective-permute-done.20 = f32[24,1024]{1,0:T(8,128)S(1)} collective-permute-done((f32[24,1024]{1,0:T(8,128)S(1)}, f32[24,1024]{1,0:T(8,128)S(1)}, u32[]{:S(2)}, u32[]{:S(2)}) %collective-permute-start.20) | collective-permute-done | bytes 98336 | tf_op jit(solution)/shard_map/ppermute | solution.py:1124
  186.9 1.3 collective-permute-start.18
  188.2 3.3 %collective-permute-done.18 = f32[24,1024]{1,0:T(8,128)S(1)} collective-permute-done((f32[24,1024]{1,0:T(8,128)S(1)}, f32[24,1024]{1,0:T(8,128)S(1)}, u32[]{:S(2)}, u32[]{:S(2)}) %collective-permute-start.18) | collective-permute-done | bytes 98336 | tf_op jit(solution)/shard_map/ppermute | solution.py:1124
  191.5 0.1 collective-permute-start.21
  191.6 1.6 collective-permute-start.12
  193.3 0.6 collective-permute-start.13
  194.0 1.3 collective-permute-start.29
  195.3 0.8 collective-permute-start.30
  196.1 1.6 collective-permute-start.22
  197.7 3.0 %collective-permute-done.22 = f32[24,1024]{1,0:T(8,128)S(1)} collective-permute-done((f32[24,1024]{1,0:T(8,128)S(1)}, f32[24,1024]{1,0:T(8,128)S(1)}, u32[]{:S(2)}, u32[]{:S(2)}) %collective-permute-start.22) | collective-permute-done | bytes 98336 | tf_op jit(solution)/shard_map/ppermute | solution.py:1124
  200.8 2.6 %collective-permute-start.23 = (f32[24,1024]{1,0:T(8,128)S(1)}, f32[24,1024]{1,0:T(8,128)S(1)}, u32[]{:S(2)}, u32[]{:S(2)}) collective-permute-start(f32[24,1024]{1,0:T(8,128)S(1)} %add.47), channel_id=1, source_target_pairs={{0,16},{1,17},{2,18},{3,19},{4,20},{5,21},{6,22},{7,23},{8,24},{9,... | collective-permute-start | bytes 294920 | tf_op jit(solution)/shard_map/ppermute | solution.py:1124
  203.4 3.0 %collective-permute-done.23 = f32[24,1024]{1,0:T(8,128)S(1)} collective-permute-done((f32[24,1024]{1,0:T(8,128)S(1)}, f32[24,1024]{1,0:T(8,128)S(1)}, u32[]{:S(2)}, u32[]{:S(2)}) %collective-permute-start.23) | collective-permute-done | bytes 98336 | tf_op jit(solution)/shard_map/ppermute | solution.py:1124
  206.4 0.8 shard_map.270
  207.2 1.9 shard_map.263
  209.1 2.3 %shard_map.269 = bf16[1,1024,1024]{2,1,0:T(8,128)(2,1)} custom-call(s32[1]{0:T(128)} %bitcast.meta_ref, f32[24,1024]{1,0:T(8,128)S(1)} %add.48.refs_0_.total_ref, bf16[256,1024]{1,0:T(8,128)(2,1)S(1)} %shard_map.268.refs_1_, bf16[256,1024]{1,0:T(8,128)(2,1)S(1)} %collective-permute-done.27.refs_2_, bf16[256,1024]{1,0:T(8,128)(2,1)S(1)} %collective-permute-done.28.refs_3_, ...), custom_call_target="tpu_custom_call" | custom-call | bytes 4194304 | tf_op jit(solution)/shard_map/pallas_call | solution.py:375
  (64 shorter events, 0.3 us)
Async XLA Ops:
  0.7 46.8 %copy-start.4 = (f32[6,1024]{1,0:T(8,128)S(1)}, f32[6,1024]{1,0:T(8,128)}, u32[]{:S(2)}) copy-start(f32[6,1024]{1,0:T(8,128)} %vec_ref.9) | copy-start | bytes 73732
  0.7 46.8 %copy-start.5 = (f32[2,4,1024]{2,1,0:T(4,128)S(1)}, f32[2,4,1024]{2,1,0:T(4,128)}, u32[]{:S(2)}) copy-start(f32[2,4,1024]{2,1,0:T(4,128)} %u_ref.1) | copy-start | bytes 98308
  0.7 46.8 %copy-start.7 = (f32[2,1024,4]{1,2,0:T(4,128)S(1)}, f32[2,1024,4]{1,2,0:T(4,128)}, u32[]{:S(2)}) copy-start(f32[2,1024,4]{1,2,0:T(4,128)} %param.28) | copy-start | bytes 98308
  0.7 46.8 %copy-start.15 = (f32[2,256]{1,0:T(2,128)S(1)}, f32[2,256]{1,0:T(2,128)}, u32[]{:S(2)}) copy-start(f32[2,256]{1,0:T(2,128)} %qvb_ref.1) | copy-start | bytes 6148
  4.0 32.1 %collective-permute-start.3 = (bf16[1,2576,256]{2,1,0:T(8,128)(2,1)}, bf16[1,2576,256]{2,1,0:T(8,128)(2,1)S(1)}, u32[]{:S(2)}, u32[]{:S(2)}) collective-permute-start(bf16[1,2576,256]{2,1,0:T(8,128)(2,1)} %get-tuple-element.56), channel_id=1, source_target_pairs={{0,1},{1,0},{2,3},{3,2},{4,5},{5,4},{6,7},{7,6},{8,9},{9,8},{10,11... | collective-permute-start | bytes 3956744 | tf_op jit(solution)/shard_map/ppermute | solution.py:1124
  7.0 30.6 %collective-permute-start.5 = (bf16[1,2576,256]{2,1,0:T(8,128)(2,1)}, bf16[1,2576,256]{2,1,0:T(8,128)(2,1)S(1)}, u32[]{:S(2)}, u32[]{:S(2)}) collective-permute-start(bf16[1,2576,256]{2,1,0:T(8,128)(2,1)} %get-tuple-element.57), channel_id=1, source_target_pairs={{0,2},{1,3},{2,0},{3,1},{4,6},{5,7},{6,4},{7,5},{8,10},{9,11},{10,... | collective-permute-start | bytes 3956744 | tf_op jit(solution)/shard_map/ppermute | solution.py:1124
  36.1 39.4 %collective-permute-start.4 = (bf16[1,2576,256]{2,1,0:T(8,128)(2,1)S(1)}, bf16[1,2576,256]{2,1,0:T(8,128)(2,1)}, u32[]{:S(2)}, u32[]{:S(2)}) collective-permute-start(bf16[1,2576,256]{2,1,0:T(8,128)(2,1)S(1)} %collective-permute-done.3.x0.xa_ref), channel_id=1, source_target_pairs={{0,4},{1,5},{2,6},{3,7},{4,0},{5,1},{6,2},{7,3},{8,12},{9,13},{10,... | collective-permute-start | bytes 3956744 | tf_op jit(solution)/shard_map/ppermute | solution.py:1124
  37.6 37.9 %copy-start.3 = (bf16[1,2576,256]{2,1,0:T(8,128)(2,1)}, bf16[1,2576,256]{2,1,0:T(8,128)(2,1)S(1)}, u32[]{:S(2)}) copy-start(bf16[1,2576,256]{2,1,0:T(8,128)(2,1)S(1)} %collective-permute-done.5.y0.ya_ref) | copy-start | bytes 3956740
  37.6 37.9 %collective-permute-start.6 = (bf16[1,2576,256]{2,1,0:T(8,128)(2,1)S(1)}, bf16[1,2576,256]{2,1,0:T(8,128)(2,1)}, u32[]{:S(2)}, u32[]{:S(2)}) collective-permute-start(bf16[1,2576,256]{2,1,0:T(8,128)(2,1)S(1)} %collective-permute-done.5.y0.ya_ref), channel_id=1, source_target_pairs={{0,4},{1,5},{2,6},{3,7},{4,0},{5,1},{6,2},{7,3},{8,12},{9,13},{10,... | collective-permute-start | bytes 3956744 | tf_op jit(solution)/shard_map/ppermute | solution.py:1124
  37.6 9.8 %collective-permute-start.7 = (bf16[128,1024]{1,0:T(8,128)(2,1)}, bf16[128,1024]{1,0:T(8,128)(2,1)S(1)}, u32[]{:S(2)}, u32[]{:S(2)}) collective-permute-start(bf16[128,1024]{1,0:T(8,128)(2,1)} %get-tuple-element.58), channel_id=1, source_target_pairs={{0,3},{1,2},{2,1},{3,0},{4,7},{5,6},{6,5},{7,4},{8,11},{9,10},{10,... | collective-permute-start | bytes 786440 | tf_op jit(solution)/shard_map/ppermute | solution.py:1124
  47.4 22.6 %collective-permute-start.8 = (bf16[128,1024]{1,0:T(8,128)(2,1)S(1)}, bf16[128,1024]{1,0:T(8,128)(2,1)S(1)}, u32[]{:S(2)}, u32[]{:S(2)}) collective-permute-start(bf16[128,1024]{1,0:T(8,128)(2,1)S(1)} %collective-permute-done.7.d0), channel_id=1, source_target_pairs={{0,4},{1,5},{2,6},{3,7},{4,0},{5,1},{6,2},{7,3},{8,12},{9,13},{10,... | collective-permute-start | bytes 786440 | tf_op jit(solution)/shard_map/ppermute | solution.py:1124
  47.5 1.4 copy-start.13
  55.5 12.5 %copy-start.16 = (bf16[1024,256]{1,0:T(8,128)(2,1)}, bf16[1024,256]{1,0:T(8,128)(2,1)S(1)}, u32[]{:S(2)}) copy-start(bf16[1024,256]{1,0:T(8,128)(2,1)S(1)} %get-tuple-element.53.v_ref) | copy-start | bytes 1572868
  55.5 16.6 %copy-start = (bf16[1024,1024]{1,0:T(8,128)(2,1)S(1)}, bf16[1024,1024]{1,0:T(8,128)(2,1)}, u32[]{:S(2)}) copy-start(bf16[1024,1024]{1,0:T(8,128)(2,1)} %wh_ref.1) | copy-start | bytes 6291460
  55.5 16.6 %copy-start.1 = (bf16[1024,1024]{1,0:T(8,128)(2,1)S(1)}, bf16[1024,1024]{1,0:T(8,128)(2,1)}, u32[]{:S(2)}) copy-start(bf16[1024,1024]{1,0:T(8,128)(2,1)} %wo_ref.1) | copy-start | bytes 6291460
  55.5 16.6 %copy-start.6 = (f32[1024]{0:T(1024)S(1)}, f32[1024]{0:T(1024)}, u32[]{:S(2)}) copy-start(f32[1024]{0:T(1024)} %param.23) | copy-start | bytes 12292
  68.0 7.6 %copy-start.18 = (f32[256,1024]{1,0:T(8,128)}, f32[256,1024]{1,0:T(8,128)S(1)}, u32[]{:S(2)}) copy-start(f32[256,1024]{1,0:T(8,128)S(1)} %get-tuple-element.63.ot_ref) | copy-start | bytes 3145732
  68.0 10.1 %collective-permute-start = (bf16[512,256]{1,0:T(8,128)(2,1)S(1)}, bf16[512,256]{1,0:T(8,128)(2,1)S(1)}, u32[]{:S(2)}, u32[]{:S(2)}) collective-permute-start(bf16[512,256]{1,0:T(8,128)(2,1)S(1)} %get-tuple-element.55), channel_id=1, source_target_pairs={{0,1},{1,0},{2,3},{3,2},{4,5},{5,4},{6,7},{7,6},{8,9},{9,8},{10,11... | collective-permute-start | bytes 786440 | tf_op jit(solution)/shard_map/ppermute | solution.py:1124
  68.3 13.3 %collective-permute-start.1 = (bf16[512,256]{1,0:T(8,128)(2,1)S(1)}, bf16[512,256]{1,0:T(8,128)(2,1)S(1)}, u32[]{:S(2)}, u32[]{:S(2)}) collective-permute-start(bf16[512,256]{1,0:T(8,128)(2,1)S(1)} %get-tuple-element.55), channel_id=1, source_target_pairs={{0,2},{1,3},{2,0},{3,1},{4,6},{5,7},{6,4},{7,5},{8,10},{9,11},{10,... | collective-permute-start | bytes 786440 | tf_op jit(solution)/shard_map/ppermute | solution.py:1124
  70.0 13.2 %collective-permute-start.2 = (bf16[512,256]{1,0:T(8,128)(2,1)S(1)}, bf16[512,256]{1,0:T(8,128)(2,1)S(1)}, u32[]{:S(2)}, u32[]{:S(2)}) collective-permute-start(bf16[512,256]{1,0:T(8,128)(2,1)S(1)} %get-tuple-element.54.ho_ref), channel_id=1, source_target_pairs={{0,3},{1,2},{2,1},{3,0},{4,7},{5,6},{6,5},{7,4},{8,11},{9,10},{10,... | collective-permute-start | bytes 786440 | tf_op jit(solution)/shard_map/ppermute | solution.py:1124
  72.2 3.4 %copy-start.2 = (bf16[256,1024]{1,0:T(8,128)(2,1)S(1)}, bf16[256,1024]{1,0:T(8,128)(2,1)}, u32[]{:S(2)}) copy-start(bf16[256,1024]{1,0:T(8,128)(2,1)} %own_ref.1) | copy-start | bytes 1572868
  75.5 7.7 %copy-start.12 = (s32[8]{0:T(128)S(1)}, s32[8]{0:T(128)}, u32[]{:S(2)}) copy-start(s32[8]{0:T(128)} %counts_ref.7) | copy-start | bytes 100
  96.7 15.3 %collective-permute-start.14 = (bf16[256,1024]{1,0:T(8,128)(2,1)S(1)}, bf16[256,1024]{1,0:T(8,128)(2,1)S(1)}, u32[]{:S(2)}, u32[]{:S(2)}) collective-permute-start(bf16[256,1024]{1,0:T(8,128)(2,1)S(1)} %get-tuple-element.65), channel_id=1, source_target_pairs={{0,3},{1,2},{2,1},{3,0},{4,7},{5,6},{6,5},{7,4},{8,11},{9,10},{10,... | collective-permute-start | bytes 1572872 | tf_op jit(solution)/shard_map/ppermute | solution.py:1124
  112.0 22.9 %copy-start.17 = (bf16[1024,256]{1,0:T(8,128)(2,1)S(1)}, bf16[1024,256]{1,0:T(8,128)(2,1)}, u32[]{:S(2)}) copy-start(bf16[1024,256]{1,0:T(8,128)(2,1)} %copy-done.16) | copy-start | bytes 1572868
  112.0 22.8 %copy-start.19 = (f32[256,1024]{1,0:T(8,128)S(1)}, f32[256,1024]{1,0:T(8,128)}, u32[]{:S(2)}) copy-start(f32[256,1024]{1,0:T(8,128)} %copy-done.18) | copy-start | bytes 3145732
  115.2 6.4 %collective-permute-start.15 = (bf16[256,256]{1,0:T(8,128)(2,1)S(1)}, bf16[256,256]{1,0:T(8,128)(2,1)S(1)}, u32[]{:S(2)}, u32[]{:S(2)}) collective-permute-start(bf16[256,256]{1,0:T(8,128)(2,1)S(1)} %get-tuple-element.67), channel_id=1, source_target_pairs={{0,1},{1,0},{2,3},{3,2},{4,5},{5,4},{6,7},{7,6},{8,9},{9,8},{10,11... | collective-permute-start | bytes 393224 | tf_op jit(solution)/shard_map/ppermute | solution.py:1124
  115.8 19.0 %collective-permute-start.16 = (bf16[256,256]{1,0:T(8,128)(2,1)S(1)}, bf16[256,256]{1,0:T(8,128)(2,1)S(1)}, u32[]{:S(2)}, u32[]{:S(2)}) collective-permute-start(bf16[256,256]{1,0:T(8,128)(2,1)S(1)} %get-tuple-element.68), channel_id=1, source_target_pairs={{0,2},{1,3},{2,0},{3,1},{4,6},{5,7},{6,4},{7,5},{8,10},{9,11},{10,... | collective-permute-start | bytes 393224 | tf_op jit(solution)/shard_map/ppermute | solution.py:1124
  117.0 17.8 %collective-permute-start.17 = (bf16[256,256]{1,0:T(8,128)(2,1)S(1)}, bf16[256,256]{1,0:T(8,128)(2,1)S(1)}, u32[]{:S(2)}, u32[]{:S(2)}) collective-permute-start(bf16[256,256]{1,0:T(8,128)(2,1)S(1)} %get-tuple-element.69), channel_id=1, source_target_pairs={{0,3},{1,2},{2,1},{3,0},{4,7},{5,6},{6,5},{7,4},{8,11},{9,10},{10,... | collective-permute-start | bytes 393224 | tf_op jit(solution)/shard_map/ppermute | solution.py:1124
  118.8 37.1 %collective-permute-start.9 = (bf16[256,1024]{1,0:T(8,128)(2,1)S(1)}, bf16[256,1024]{1,0:T(8,128)(2,1)S(1)}, u32[]{:S(2)}, u32[]{:S(2)}) collective-permute-start(bf16[256,1024]{1,0:T(8,128)(2,1)S(1)} %get-tuple-element.61), channel_id=1, source_target_pairs={{0,3},{1,2},{2,1},{3,0},{4,7},{5,6},{6,5},{7,4},{8,11},{9,10},{10,... | collective-permute-start | bytes 1572872 | tf_op jit(solution)/shard_map/ppermute | solution.py:1124
  134.8 10.4 %copy-start.14 = (bf16[3,1024,256]{2,1,0:T(8,128)(2,1)S(1)}, bf16[3,1024,256]{2,1,0:T(8,128)(2,1)}, u32[]{:S(2)}) copy-start(bf16[3,1024,256]{2,1,0:T(8,128)(2,1)} %w_ref.3) | copy-start | bytes 4718596
  149.0 14.9 %collective-permute-start.24 = (bf16[256,1024]{1,0:T(8,128)(2,1)S(1)}, bf16[256,1024]{1,0:T(8,128)(2,1)S(1)}, u32[]{:S(2)}, u32[]{:S(2)}) collective-permute-start(bf16[256,1024]{1,0:T(8,128)(2,1)S(1)} %get-tuple-element.76), channel_id=1, source_target_pairs={{0,1},{1,0},{2,3},{3,2},{4,5},{5,4},{6,7},{7,6},{8,9},{9,8},{10,11... | collective-permute-start | bytes 1572872 | tf_op jit(solution)/shard_map/ppermute | solution.py:1124
  150.1 15.6 %collective-permute-start.25 = (bf16[256,1024]{1,0:T(8,128)(2,1)S(1)}, bf16[256,1024]{1,0:T(8,128)(2,1)S(1)}, u32[]{:S(2)}, u32[]{:S(2)}) collective-permute-start(bf16[256,1024]{1,0:T(8,128)(2,1)S(1)} %get-tuple-element.77), channel_id=1, source_target_pairs={{0,2},{1,3},{2,0},{3,1},{4,6},{5,7},{6,4},{7,5},{8,10},{9,11},{10,... | collective-permute-start | bytes 1572872 | tf_op jit(solution)/shard_map/ppermute | solution.py:1124
  151.2 22.1 %collective-permute-start.26 = (bf16[256,1024]{1,0:T(8,128)(2,1)S(1)}, bf16[256,1024]{1,0:T(8,128)(2,1)S(1)}, u32[]{:S(2)}, u32[]{:S(2)}) collective-permute-start(bf16[256,1024]{1,0:T(8,128)(2,1)S(1)} %get-tuple-element.78), channel_id=1, source_target_pairs={{0,3},{1,2},{2,1},{3,0},{4,7},{5,6},{6,5},{7,4},{8,11},{9,10},{10,... | collective-permute-start | bytes 1572872 | tf_op jit(solution)/shard_map/ppermute | solution.py:1124
  155.1 22.6 %collective-permute-start.19 = (f32[24,1024]{1,0:T(8,128)S(1)}, f32[24,1024]{1,0:T(8,128)S(1)}, u32[]{:S(2)}, u32[]{:S(2)}) collective-permute-start(f32[24,1024]{1,0:T(8,128)S(1)} %shard_map.266), channel_id=1, source_target_pairs={{0,2},{1,3},{2,0},{3,1},{4,6},{5,7},{6,4},{7,5},{8,10},{9,11},{10,... | collective-permute-start | bytes 294920 | tf_op jit(solution)/shard_map/ppermute | solution.py:1124
  156.2 35.4 %collective-permute-start.10 = (bf16[256,1024]{1,0:T(8,128)(2,1)S(1)}, bf16[256,1024]{1,0:T(8,128)(2,1)S(1)}, u32[]{:S(2)}, u32[]{:S(2)}) collective-permute-start(bf16[256,1024]{1,0:T(8,128)(2,1)S(1)} %add_convert_fusion.refs_0_), channel_id=1, source_target_pairs={{0,1},{1,0},{2,3},{3,2},{4,5},{5,4},{6,7},{7,6},{8,9},{9,8},{10,11... | collective-permute-start | bytes 1572872 | tf_op jit(solution)/shard_map/ppermute | solution.py:1124
  163.9 29.4 %collective-permute-start.11 = (bf16[256,1024]{1,0:T(8,128)(2,1)S(1)}, bf16[256,1024]{1,0:T(8,128)(2,1)S(1)}, u32[]{:S(2)}, u32[]{:S(2)}) collective-permute-start(bf16[256,1024]{1,0:T(8,128)(2,1)S(1)} %add_convert_fusion.refs_0_), channel_id=1, source_target_pairs={{0,2},{1,3},{2,0},{3,1},{4,6},{5,7},{6,4},{7,5},{8,10},{9,11},{10,... | collective-permute-start | bytes 1572872 | tf_op jit(solution)/shard_map/ppermute | solution.py:1124
  175.2 31.2 %copy-start.8 = (f32[2,1024,4]{1,2,0:T(4,128)S(1)}, f32[2,1024,4]{1,2,0:T(4,128)}, u32[]{:S(2)}) copy-start(f32[2,1024,4]{1,2,0:T(4,128)} %param.30) | copy-start | bytes 98308
  175.2 31.2 %copy-start.9 = (f32[2,4,1024]{2,1,0:T(4,128)S(1)}, f32[2,4,1024]{2,1,0:T(4,128)}, u32[]{:S(2)}) copy-start(f32[2,4,1024]{2,1,0:T(4,128)} %mu_ref.1) | copy-start | bytes 98308
  175.2 31.2 %copy-start.10 = (f32[2,1024,4]{1,2,0:T(4,128)S(1)}, f32[2,1024,4]{1,2,0:T(4,128)}, u32[]{:S(2)}) copy-start(f32[2,1024,4]{1,2,0:T(4,128)} %param.32) | copy-start | bytes 98308
  175.2 31.2 %copy-start.11 = (f32[2,4,1024]{2,1,0:T(4,128)S(1)}, f32[2,4,1024]{2,1,0:T(4,128)}, u32[]{:S(2)}) copy-start(f32[2,4,1024]{2,1,0:T(4,128)} %au_ref.1) | copy-start | bytes 98308
  175.2 18.7 %collective-permute-start.27 = (bf16[256,1024]{1,0:T(8,128)(2,1)S(1)}, bf16[256,1024]{1,0:T(8,128)(2,1)S(1)}, u32[]{:S(2)}, u32[]{:S(2)}) collective-permute-start(bf16[256,1024]{1,0:T(8,128)(2,1)S(1)} %shard_map.268.refs_1_), channel_id=1, source_target_pairs={{0,1},{1,0},{2,3},{3,2},{4,5},{5,4},{6,7},{7,6},{8,9},{9,8},{10,11... | collective-permute-start | bytes 1572872 | tf_op jit(solution)/shard_map/ppermute | solution.py:1124
  176.9 18.4 %collective-permute-start.28 = (bf16[256,1024]{1,0:T(8,128)(2,1)S(1)}, bf16[256,1024]{1,0:T(8,128)(2,1)S(1)}, u32[]{:S(2)}, u32[]{:S(2)}) collective-permute-start(bf16[256,1024]{1,0:T(8,128)(2,1)S(1)} %shard_map.268.refs_1_), channel_id=1, source_target_pairs={{0,2},{1,3},{2,0},{3,1},{4,6},{5,7},{6,4},{7,5},{8,10},{9,11},{10,... | collective-permute-start | bytes 1572872 | tf_op jit(solution)/shard_map/ppermute | solution.py:1124
  177.7 9.2 %collective-permute-start.20 = (f32[24,1024]{1,0:T(8,128)S(1)}, f32[24,1024]{1,0:T(8,128)S(1)}, u32[]{:S(2)}, u32[]{:S(2)}) collective-permute-start(f32[24,1024]{1,0:T(8,128)S(1)} %shard_map.266), channel_id=1, source_target_pairs={{0,3},{1,2},{2,1},{3,0},{4,7},{5,6},{6,5},{7,4},{8,11},{9,10},{10,... | collective-permute-start | bytes 294920 | tf_op jit(solution)/shard_map/ppermute | solution.py:1124
  186.9 4.6 %collective-permute-start.18 = (f32[24,1024]{1,0:T(8,128)S(1)}, f32[24,1024]{1,0:T(8,128)S(1)}, u32[]{:S(2)}, u32[]{:S(2)}) collective-permute-start(f32[24,1024]{1,0:T(8,128)S(1)} %shard_map.266), channel_id=1, source_target_pairs={{0,1},{1,0},{2,3},{3,2},{4,5},{5,4},{6,7},{7,6},{8,9},{9,8},{10,11... | collective-permute-start | bytes 294920 | tf_op jit(solution)/shard_map/ppermute | solution.py:1124
  191.5 4.5 %collective-permute-start.21 = (f32[24,1024]{1,0:T(8,128)S(1)}, f32[24,1024]{1,0:T(8,128)S(1)}, u32[]{:S(2)}, u32[]{:S(2)}) collective-permute-start(f32[24,1024]{1,0:T(8,128)S(1)} %add_add_fusion), channel_id=1, source_target_pairs={{0,4},{1,5},{2,6},{3,7},{4,0},{5,1},{6,2},{7,3},{8,12},{9,13},{10,... | collective-permute-start | bytes 294920 | tf_op jit(solution)/shard_map/ppermute | solution.py:1124
  191.6 15.5 %collective-permute-start.12 = (bf16[128,1024]{1,0:T(8,128)(2,1)S(1)}, bf16[128,1024]{1,0:T(8,128)(2,1)S(1)}, u32[]{:S(2)}, u32[]{:S(2)}) collective-permute-start(bf16[128,1024]{1,0:T(8,128)(2,1)S(1)} %slice.20), channel_id=1, source_target_pairs={{0,2},{1,3},{2,0},{3,1},{4,6},{5,7},{6,4},{7,5},{8,10},{9,11},{10,... | collective-permute-start | bytes 786440 | tf_op jit(solution)/shard_map/ppermute | solution.py:1124
  193.3 13.9 %collective-permute-start.13 = (bf16[128,1024]{1,0:T(8,128)(2,1)S(1)}, bf16[128,1024]{1,0:T(8,128)(2,1)S(1)}, u32[]{:S(2)}, u32[]{:S(2)}) collective-permute-start(bf16[128,1024]{1,0:T(8,128)(2,1)S(1)} %slice.21), channel_id=1, source_target_pairs={{0,1},{1,0},{2,3},{3,2},{4,5},{5,4},{6,7},{7,6},{8,9},{9,8},{10,11... | collective-permute-start | bytes 786440 | tf_op jit(solution)/shard_map/ppermute | solution.py:1124
  194.0 15.1 %collective-permute-start.29 = (bf16[128,1024]{1,0:T(8,128)(2,1)S(1)}, bf16[128,1024]{1,0:T(8,128)(2,1)S(1)}, u32[]{:S(2)}, u32[]{:S(2)}) collective-permute-start(bf16[128,1024]{1,0:T(8,128)(2,1)S(1)} %slice.22), channel_id=1, source_target_pairs={{0,2},{1,3},{2,0},{3,1},{4,6},{5,7},{6,4},{7,5},{8,10},{9,11},{10,... | collective-permute-start | bytes 786440 | tf_op jit(solution)/shard_map/ppermute | solution.py:1124
  195.3 13.8 %collective-permute-start.30 = (bf16[128,1024]{1,0:T(8,128)(2,1)S(1)}, bf16[128,1024]{1,0:T(8,128)(2,1)S(1)}, u32[]{:S(2)}, u32[]{:S(2)}) collective-permute-start(bf16[128,1024]{1,0:T(8,128)(2,1)S(1)} %slice.23), channel_id=1, source_target_pairs={{0,1},{1,0},{2,3},{3,2},{4,5},{5,4},{6,7},{7,6},{8,9},{9,8},{10,11... | collective-permute-start | bytes 786440 | tf_op jit(solution)/shard_map/ppermute | solution.py:1124
  196.1 4.7 %collective-permute-start.22 = (f32[24,1024]{1,0:T(8,128)S(1)}, f32[24,1024]{1,0:T(8,128)S(1)}, u32[]{:S(2)}, u32[]{:S(2)}) collective-permute-start(f32[24,1024]{1,0:T(8,128)S(1)} %add.46), channel_id=1, source_target_pairs={{0,8},{1,9},{2,10},{3,11},{4,12},{5,13},{6,14},{7,15},{8,0},{9,1},... | collective-permute-start | bytes 294920 | tf_op jit(solution)/shard_map/ppermute | solution.py:1124
  200.8 5.6 %collective-permute-start.23 = (f32[24,1024]{1,0:T(8,128)S(1)}, f32[24,1024]{1,0:T(8,128)S(1)}, u32[]{:S(2)}, u32[]{:S(2)}) collective-permute-start(f32[24,1024]{1,0:T(8,128)S(1)} %add.47), channel_id=1, source_target_pairs={{0,16},{1,17},{2,18},{3,19},{4,20},{5,21},{6,22},{7,23},{8,24},{9,... | collective-permute-start | bytes 294920 | tf_op jit(solution)/shard_map/ppermute | solution.py:1124
where the time goes:
time: 212 us; the launch traced here: 211 us
  waiting for transfers between devices  89.5 us (42%)
  Pallas kernels  81.9 us (39%)
  starting transfers between devices  36.3 us (17%)
    ppermute x31, waiting for transfers between devices, send(): return lax.ppermute(value, axes, pairs)  89.5 us
    pallas_call x15, Pallas kernels, call(): pl.pallas_call(kernel, grid_spec=pltpu.PrefetchScalarGridSpec(num_scalar_...  81.9 us
    ppermute x31, starting transfers between devices, send(): return lax.ppermute(value, axes, pairs)  36.3 us
  transfers between devices with their start and end apart: 31, of which 14 were waited for; matrix products, arithmetic and copies ran while one was open for 0% of the time, Pallas kernels for 28%

commit v1 on v0

--- a/solution.py
+++ b/solution.py
@@ -370,7 +370,8 @@
 
 
 def call(
-    kernel, grid, in_specs, out_specs, out_shape, args, prefetch, scratch=(), est=None, vmem=48
+    kernel, grid, in_specs, out_specs, out_shape, args, prefetch, scratch=(), est=None, vmem=20,
+    alias=None,
 ):
     return pl.pallas_call(
         kernel,
@@ -383,6 +384,7 @@
         ),
         out_shape=out_shape,
         cost_estimate=est,
+        input_output_aliases=alias or {},
         compiler_params=pltpu.CompilerParams(vmem_limit_bytes=vmem * 1024 * 1024),
     )(*prefetch, *args)
 
@@ -391,45 +393,69 @@
     return jax.ShapeDtypeStruct(shape, dtype)
 
 
-def fill_pack(out_ref, wh_ref, wo_ref, hb_ref):
-    width = wh_ref.shape[0]
-    out_ref[0, 0:width, :] = wh_ref[...]
-    for j in range(width // QUARTER):
-        out_ref[0, width + QUARTER * j : width + QUARTER * (j + 1), :] = wo_ref[
-            :, QUARTER * j : QUARTER * (j + 1)
-        ]
-    bias = hb_ref[...]
+def bias_rows(bias):
     high = bias.astype(BF16)
     rest = bias - high.astype(F32)
     mid = rest.astype(BF16)
     low = (rest - mid.astype(F32)).astype(BF16)
-    row = lax.broadcasted_iota(jnp.int32, (BIAS_ROWS, QUARTER), 0)
-    spread = lambda v: jnp.broadcast_to(v.astype(F32), (BIAS_ROWS, QUARTER))
+    shape = (BIAS_ROWS, bias.shape[1])
+    row = lax.broadcasted_iota(jnp.int32, shape, 0)
+    spread = lambda v: jnp.broadcast_to(v.astype(F32), shape)
     packed = jnp.where(row == 0, spread(high), jnp.where(row == 1, spread(mid), spread(low)))
-    out_ref[0, 2 * width : 2 * width + BIAS_ROWS, :] = jnp.where(row < 3, packed, 0.0).astype(BF16)
-
-
-def pack_kernel(which_ref, wh_ref, wo_ref, hb_ref, out_ref):
-    fill_pack(out_ref, wh_ref, wo_ref, hb_ref)
-
-
-def fetch_kernel(core_ref, whx, wox, hbx, why, woy, hby, proj_ref, x_ref, y_ref, d_ref):
-    width = whx.shape[0]
+    return jnp.where(row < 3, packed, 0.0).astype(BF16)
+
+
+def turned(block):
+    return block.astype(F32).T.astype(BF16)
+
+
+def pack_kernel(wh_ref, wo_ref, hb_ref, out_ref):
+    units = wo_ref.shape[0]
+    out_ref[0, 0:units, :] = turned(wh_ref[...])
+    out_ref[0, units : 2 * units, :] = wo_ref[...]
+    for n in range(units // LANES):
+        base = 2 * units + BIAS_ROWS * n
+        out_ref[0, base : base + BIAS_ROWS, 0:LANES] = bias_rows(
+            hb_ref[:, LANES * n : LANES * (n + 1)]
+        )
+
+
+def pack(hidden_weight, hidden_output_weight, hidden_bias):
+    width, hidden = hidden_weight.shape
+    count = hidden // QUARTER
+    rows = 2 * QUARTER + BIAS_ROWS * (QUARTER // LANES)
+    return call(
+        pack_kernel,
+        (count,),
+        [
+            pl.BlockSpec((width, QUARTER), lambda i: (0, i)),
+            pl.BlockSpec((QUARTER, width), lambda i: (i, 0)),
+            pl.BlockSpec((1, QUARTER), lambda i: (0, i)),
+        ],
+        pl.BlockSpec((1, rows, width), lambda i: (i, 0, 0)),
+        sds((count, rows, width), BF16),
+        (hidden_weight, hidden_output_weight, hidden_bias.reshape(1, -1)),
+        (),
+        est=cost(0, 4 * rows * width * count),
+    )
+
+
+def fetch_kernel(core_ref, whx, wox, hbx, why, woy, hby, proj_ref, xa_ref, xb_ref, ya_ref, yb_ref):
     half = proj_ref.shape[0]
-    for ref, ops in ((x_ref, (whx, wox, hbx)), (y_ref, (why, woy, hby))):
-        fill_pack(ref, *ops)
-        for j in range(width // QUARTER):
-            base = 2 * width + BIAS_ROWS + half * j
-            ref[0, base : base + half, :] = proj_ref[:, QUARTER * j : QUARTER * (j + 1)]
-    d_ref[...] = proj_ref[...]
+    for refs, wh, wo, hb in (((xa_ref, xb_ref), whx, wox, hbx), ((ya_ref, yb_ref), why, woy, hby)):
+        for n, ref in enumerate(refs):
+            at = slice(LANES * n, LANES * (n + 1))
+            ref[0:LANES, :] = turned(wh[:, at])
+            ref[LANES : 2 * LANES, :] = wo[at, :]
+            ref[2 * LANES : 2 * LANES + BIAS_ROWS, 0:LANES] = bias_rows(hb[:, at])
+        refs[0][2 * LANES + BIAS_ROWS : 2 * LANES + BIAS_ROWS + half, :] = proj_ref[...]
 
 
 def fetch_packs(core, hidden_weight, hidden_output_weight, hidden_bias, projection):
     width = hidden_weight.shape[0]
     half = projection.shape[0] // 2
-    rows = 2 * width + BIAS_ROWS + half * (width // QUARTER)
-    bias = hidden_bias.reshape(1, -1)
-    triple = (hidden_weight, hidden_output_weight, bias)
+    rows = 2 * LANES + BIAS_ROWS
+    triple = (hidden_weight, hidden_output_weight, hidden_bias.reshape(1, -1))
     specs = []
     for base in (0, 2):
         specs += [
@@ -437,35 +463,17 @@
             pl.BlockSpec((QUARTER, width), lambda i, c, base=base: (base + c[0], 0)),
             pl.BlockSpec((1, QUARTER), lambda i, c, base=base: (0, base + c[0])),
         ]
+    shapes = [(rows + half, width), (rows, width)] * 2
     return call(
         fetch_kernel,
         (1,),
         specs + [pl.BlockSpec((half, width), lambda i, c: (c[0], 0))],
-        [whole((1, rows, QUARTER)), whole((1, rows, QUARTER)), whole((half, width))],
-        [sds((1, rows, QUARTER), BF16)] * 2 + [sds((half, width), BF16)],
+        [whole(shape) for shape in shapes],
+        [sds(shape, BF16) for shape in shapes],
         (*triple, *triple, projection),
         (core,),
-        est=cost(0, 8 * rows * QUARTER),
+        est=cost(0, 16 * rows * width),
         vmem=62,
-    )
-
-
-def pack(which, count, hidden_weight, hidden_output_weight, hidden_bias):
-    width = hidden_weight.shape[0]
-    rows = 2 * width + BIAS_ROWS
-    return call(
-        pack_kernel,
-        (count,),
-        [
-            pl.BlockSpec((width, QUARTER), lambda i, w: (0, w[i])),
-            pl.BlockSpec((QUARTER, width), lambda i, w: (w[i], 0)),
-            pl.BlockSpec((1, QUARTER), lambda i, w: (0, w[i])),
-        ],
-        pl.BlockSpec((1, rows, QUARTER), lambda i, w: (i, 0, 0)),
-        sds((count, rows, QUARTER), BF16),
-        (hidden_weight, hidden_output_weight, hidden_bias.reshape(1, -1)),
-        (which,),
-        est=cost(0, 4 * rows * QUARTER * count),
     )
 
 
@@ -669,134 +677,186 @@
     )
 
 
-def mlp_kernel(
-    meta_ref, groups_ref, counts_ref, x_ref, cot_ref, vec_ref,
-    ho_ref, hx_ref, hy_ref, hd_ref, wof_ref,
-    own_ref, xa_ref, xb_ref, ya_ref, yb_ref,
-    gn_ref, mlp_ref, resid_ref, n2_s, low_s, h_s, gn_s, mlp_s, buf, sem,
-):
-    width = x_ref.shape[2]
-    blocks = own_ref.shape[0]
-    total = blocks + 4
-    extras = (xa_ref, xb_ref, ya_ref, yb_ref)
-    depth = own_ref.shape[1]
+def mlp_kernel(enter, leave, has_own, n_pairs, *refs):
+    refs = list(refs)
+    meta_ref = refs.pop(0)
+
+    def take(n):
+        out = refs[:n]
+        del refs[:n]
+        return out
+
+    if enter:
+        groups_ref, counts_ref, x_ref, cot_ref, vec_ref, *head_refs, wof_ref = take(10)
+    else:
+        n2_in, low_in, gn_in, mlp_in = take(4)
+    own_refs = take(1) if has_own else []
+    pairs = [take(2) for _ in range(n_pairs)]
+    if leave:
+        outs = take(3 if enter else 2)
+    else:
+        outs = take(4)
+    n2_s, low_s, h_s, gn_s, mlp_s, act_s, pre_s, buf, sem = refs
+    blocks = own_refs[0].shape[0] if has_own else 0
+    total = blocks + n_pairs
+    depth = buf.shape[1]
 
     def fetch(i, slot):
-        @pl.when(i < blocks)
-        def _():
-            pltpu.make_async_copy(own_ref.at[jnp.minimum(i, blocks - 1)], buf.at[slot], sem.at[slot]).start()
-
-        for n, ref in enumerate(extras):
+        if has_own:
+            @pl.when(i < blocks)
+            def _():
+                at = jnp.minimum(i, blocks - 1)
+                pltpu.make_async_copy(own_refs[0].at[at], buf.at[slot], sem.at[slot]).start()
+
+        for n, two in enumerate(pairs):
             @pl.when(i == blocks + n)
-            def _(ref=ref):
-                pltpu.make_async_copy(ref.at[0, 0:depth], buf.at[slot], sem.at[slot]).start()
+            def _(two=two):
+                for m, ref in enumerate(two):
+                    for part, rows in ((0, LANES), (LANES, LANES), (2 * LANES, BIAS_ROWS)):
+                        pltpu.make_async_copy(
+                            ref.at[pl.ds(part, rows)],
+                            buf.at[slot, pl.ds(2 * part + m * rows, rows)],
+                            sem.at[slot],
+                        ).start()
+
+    def settle(slot):
+        pltpu.make_async_copy(buf.at[slot], buf.at[slot], sem.at[slot]).wait()
 
     fetch(0, 0)
-    local = ho_ref.shape[1]
-    for n, ref in enumerate((ho_ref, hx_ref, hy_ref, hd_ref)):
-        h_s[:, local * n : local * (n + 1)] = ref[...]
-    resid = x_ref[0].astype(F32) + dot(h_s[...], wof_ref[...]) + vec_ref[4:5, :]
-    resid_ref[...] = resid
-    xhat, _ = rows_stats(resid)
-    n2_s[...] = (xhat * vec_ref[2:3, :] + vec_ref[3:4, :]).astype(BF16)
-    weight = seq_weight_of(groups_ref, counts_ref)[:, 0:1]
-    low_s[...] = (cot_ref[0].astype(F32) * weight).astype(BF16)
-    gn_s[...] = jnp.zeros_like(gn_s)
-    mlp_s[...] = jnp.zeros_like(mlp_s)
-
-    @pl.loop(0, total)
-    def _(i):
-        slot = i & 1
-        pltpu.make_async_copy(own_ref.at[0], buf.at[slot], sem.at[slot]).wait()
-
-        @pl.when(i + 1 < total)
-        def _():
-            fetch(i + 1, 1 - slot)
-
-        wh = buf[slot, 0:width, :]
-        tail = buf[slot, 2 * width : 2 * width + BIAS_ROWS, :].astype(F32)
-        bias = tail[0:1, :] + tail[1:2, :] + tail[2:3, :]
-        pre = dot(n2_s[...], wh) + bias
-        grad_act = jnp.zeros_like(pre)
-        for j in range(width // QUARTER):
-            piece = buf[slot, width + QUARTER * j : width + QUARTER * (j + 1), :]
-            grad_act = grad_act + dot_nt(low_s[:, QUARTER * j : QUARTER * (j + 1)], piece)
+    if enter:
+        local = head_refs[0].shape[1]
+        for n, ref in enumerate(head_refs):
+            h_s[:, local * n : local * (n + 1)] = ref[...]
+        resid = x_ref[0].astype(F32) + dot(h_s[...], wof_ref[...]) + vec_ref[4:5, :]
+        if leave:
+            outs[2][...] = resid
+        xhat, _ = rows_stats(resid)
+        n2_s[...] = (xhat * vec_ref[2:3, :] + vec_ref[3:4, :]).astype(BF16)
+        weight = seq_weight_of(groups_ref, counts_ref)[:, 0:1]
+        low_s[...] = (cot_ref[0].astype(F32) * weight).astype(BF16)
+        gn_s[...] = jnp.zeros_like(gn_s)
+        mlp_s[...] = jnp.zeros_like(mlp_s)
+    else:
+        n2_s[...] = n2_in[...]
+        low_s[...] = low_in[...]
+        gn_s[...] = gn_in[...]
+        mlp_s[...] = mlp_in[...]
+
+    def ahead(slot):
+        tail = buf[slot, 2 * QUARTER : depth, 0:LANES].astype(F32)
+        parts = [
+            tail[n : n + 1, :] + tail[n + 1 : n + 2, :] + tail[n + 2 : n + 3, :]
+            for n in range(0, depth - 2 * QUARTER, BIAS_ROWS)
+        ]
+        pre = dot_nt(n2_s[...], buf[slot, 0:QUARTER, :]) + jnp.concatenate(parts, axis=1)
+        grad_act = dot_nt(low_s[...], buf[slot, QUARTER : 2 * QUARTER, :])
         root = math.sqrt(2.0 / math.pi)
         square = pre * pre
         turn = jnp.tanh(root * (pre + 0.044715 * (square * pre)))
-        act = (0.5 * pre * (1.0 + turn)).astype(BF16)
-        slope = 0.5 * (1.0 + turn) + 0.5 * pre * (1.0 - turn * turn) * (
-            root * (1.0 + 3.0 * 0.044715 * square)
-        )
-        grad_pre = (grad_act * slope).astype(BF16)
-        gn_s[...] += dot_nt(grad_pre, wh)
-        for j in range(width // QUARTER):
-            piece = buf[slot, width + QUARTER * j : width + QUARTER * (j + 1), :]
-            mlp_s[:, QUARTER * j : QUARTER * (j + 1)] += dot(act, piece)
-
-    gn_ref[...] = gn_s[...].astype(gn_ref.dtype)
-    mlp_ref[...] = mlp_s[...].astype(mlp_ref.dtype)
-
-
-def mlp_fast(final, meta, groups, counts, x, cot, vec, heads, wof, packs):
-    width = x.shape[2]
-    local = heads[0].shape[1]
-    kind = F32 if final else BF16
-    flip = 0 if final else 3
+        half = 0.5 * (1.0 + turn)
+        slope = half + (0.5 * root) * pre * (1.0 - turn * turn) * (1.0 + 3.0 * 0.044715 * square)
+        return (pre * half).astype(BF16), (grad_act * slope).astype(BF16)
+
+    def behind(slot, act, grad_pre):
+        gn_s[...] += dot(grad_pre, buf[slot, 0:QUARTER, :])
+        mlp_s[...] += dot(act, buf[slot, QUARTER : 2 * QUARTER, :])
+
+    settle(0)
+    if total > 1:
+        fetch(1, 1)
+    act_s[0], pre_s[0] = ahead(0)
+
+    @pl.loop(1, total)
+    def _(i):
+        slot = lax.rem(i, 3)
+        settle(slot)
+
+        @pl.when(i + 1 < total)
+        def _():
+            fetch(i + 1, lax.rem(i + 1, 3))
+
+        old = (i + 1) & 1
+        act, grad_pre = act_s[old], pre_s[old]
+        new_act, new_pre = ahead(slot)
+        behind(lax.rem(i + 2, 3), act, grad_pre)
+        act_s[i & 1], pre_s[i & 1] = new_act, new_pre
+
+    last = total - 1
+    behind(last % 3, act_s[last & 1], pre_s[last & 1])
+    if not leave:
+        outs[2][...] = n2_s[...]
+        outs[3][...] = low_s[...]
+    outs[0][...] = gn_s[...].astype(outs[0].dtype)
+    outs[1][...] = mlp_s[...].astype(outs[1].dtype)
+
+
+def mlp_call(meta, flip, entry, state, own, pairs, leave):
+    width = pairs[0][0].shape[1]
+    enter = entry is not None
     rows = pl.BlockSpec((1, QUARTER, width), lambda i, m: (0, tok_block((m[0] & 3) ^ flip), 0))
-    head = pl.BlockSpec((QUARTER, local), lambda i, m: ((((m[0] & 3) ^ flip) >> 1) & 1, 0))
+    out = whole((QUARTER, width))
     any_ = pl.BlockSpec(memory_space=pl.ANY)
-    out = whole((QUARTER, width))
-    depth = 2 * width + BIAS_ROWS
-    hidden = QUARTER * (packs[0].shape[0] + 4)
+    local = width // 4
+    if enter:
+        groups, counts, x, cot, vec, heads, wof = entry
+        head = pl.BlockSpec((QUARTER, local), lambda i, m: ((((m[0] & 3) ^ flip) >> 1) & 1, 0))
+        specs = [smem(), smem(), rows, rows, whole(vec.shape)] + [head] * 4 + [whole(wof.shape)]
+        args = [groups, counts, x, cot, vec, *heads, wof]
+    else:
+        specs = [out] * 4
+        args = list(state)
+    mine = [] if own is None else [own]
+    flat = [ref for two in pairs for ref in two]
+    if leave:
+        kinds = [F32, F32, F32] if enter else [BF16, BF16]
+    else:
+        kinds = [F32, F32, BF16, BF16]
+    depth = 2 * QUARTER + BIAS_ROWS * (QUARTER // LANES)
+    hidden = QUARTER * ((0 if own is None else own.shape[0]) + len(pairs))
     return call(
-        mlp_kernel,
+        functools.partial(mlp_kernel, enter, leave, own is not None, len(pairs)),
         (1,),
-        [smem(), smem(), rows, rows, whole(vec.shape), head, head, head, head, whole(wof.shape)]
-        + [any_] * 5,
-        [out, out, out],
-        [sds((QUARTER, width), kind), sds((QUARTER, width), kind), sds((QUARTER, width), F32)],
-        (groups, counts, x, cot, vec, *heads, wof, *packs),
+        specs + [any_] * (len(mine) + len(flat)),
+        [out] * len(kinds),
+        [sds((QUARTER, width), kind) for kind in kinds],
+        (*args, *mine, *flat),
         (meta,),
         scratch=[
             pltpu.VMEM((QUARTER, width), BF16),
             pltpu.VMEM((QUARTER, width), BF16),
-            pltpu.VMEM((QUARTER, 4 * local), BF16),
+            pltpu.VMEM((QUARTER, width), BF16),
             pltpu.VMEM((QUARTER, width), F32),
             pltpu.VMEM((QUARTER, width), F32),
-            pltpu.VMEM((2, depth, QUARTER), BF16),
-            pltpu.SemaphoreType.DMA((2,)),
+            pltpu.VMEM((2, QUARTER, QUARTER), BF16),
+            pltpu.VMEM((2, QUARTER, QUARTER), BF16),
+            pltpu.VMEM((3, depth, width), BF16),
+            pltpu.SemaphoreType.DMA((3,)),
         ],
         est=cost(
-            8 * QUARTER * width * hidden + 2 * QUARTER * width * width,
+            8 * QUARTER * width * hidden + (2 * QUARTER * width * width if enter else 0),
             4 * width * hidden + 2 * width * width + 16 * QUARTER * width,
             QUARTER * hidden,
         ),
     )
 
 
-def project_kernel(meta_ref, own_ref, x0, x1, y0, y1, d0, d1, wof_ref):
+def project_kernel(meta_ref, own_ref, *refs):
+    wof_ref = refs[-1]
     core = (meta_ref[0] >> 2) & 1
-    local, width = own_ref.shape
+    local = own_ref.shape[0]
     half = local // 2
     wof_ref[0:local, :] = own_ref[...]
-    for n, (first, second) in enumerate(((x0, x1), (y0, y1), (d0, d1))):
-        for ref, at in ((first, core), (second, 1 - core)):
+    for n in range(3):
+        for ref, at in ((refs[2 * n], core), (refs[2 * n + 1], 1 - core)):
             start = pl.multiple_of(local * (n + 1) + at * half, half)
-            if n == 2:
-                wof_ref[pl.ds(start, half), :] = ref[...]
-            else:
-                for j in range(width // QUARTER):
-                    wof_ref[pl.ds(start, half), QUARTER * j : QUARTER * (j + 1)] = ref[
-                        0, BIAS_ROWS + half * j : BIAS_ROWS + half * (j + 1), :
-                    ]
+            wof_ref[pl.ds(start, half), :] = ref[...]
 
 
 def project(meta, own, packs, halves):
     local, width = own.shape
-    depth = packs[0].shape[1]
-    size = depth - 2 * width
-    tail = pl.BlockSpec((pl.Element(1), pl.Element(size), pl.Element(QUARTER)), lambda i, m: (0, 2 * width, 0))
+    half = local // 2
+    skip = packs[0].shape[0] - half
+    tail = pl.BlockSpec((pl.Element(half), pl.Element(width)), lambda i, m: (skip, 0))
     return call(
         project_kernel,
         (1,),
@@ -1022,41 +1082,61 @@
     )
 
 
-def gather_kernel(scaled, meta_ref, *refs):
-    out_ref = refs[-1]
-    pieces = refs[:-1]
+def gather_kernel(scaled, first, meta_ref, *refs):
+    refs = list(refs)
+    if not first:
+        refs.pop(0)
     if scaled:
-        factor = scaled / refs[0][0:1, 0:1]
-        pieces = refs[1:-1]
-    i = pl.program_id(0)
-    for n in range(4):
-        parts = pieces[3:] if n == 3 else pieces[n : n + 1]
-
-        @pl.when(i == n)
-        def _(parts=parts):
-            start = 0
-            for ref in parts:
-                rows = ref.shape[0]
-                value = ref[...]
-                if scaled:
-                    value = (value.astype(F32) * factor).astype(BF16)
-                out_ref[0, start : start + rows, :] = value
-                start += rows
+        factor = scaled / refs.pop(0)[0:1, 0:1]
+    out_ref = refs.pop()
+
+    def put(start, ref):
+        value = ref[...]
+        if scaled:
+            value = (value.astype(F32) * factor).astype(BF16)
+        out_ref[0, start : start + ref.shape[0], :] = value
+
+    if first:
+        for n, ref in enumerate(refs):
+            @pl.when(pl.program_id(0) == n)
+            def _(ref=ref):
+                put(0, ref)
+    else:
+        put(0, refs[0])
+        put(refs[0].shape[0], refs[1])
 
 
 def gather_rows(meta, pieces, scaled=0.0, total=None):
     width = pieces[0].shape[1]
     extra = [total] if scaled else []
     specs = [pl.BlockSpec((8, width), lambda i, m: (total.shape[0] // 8 - 1, 0))] if scaled else []
+    result = sds((1, 4 * QUARTER, width), BF16)
+
+    def out(base):
+        return pl.BlockSpec(
+            (1, QUARTER, width), lambda i, m: (0, tok_block((m[0] & 3) ^ (base + i)), 0)
+        )
+
+    part = call(
+        functools.partial(gather_kernel, scaled, True),
+        (3,),
+        specs + [whole(p.shape) for p in pieces[:3]],
+        out(0),
+        result,
+        (*extra, *pieces[:3]),
+        (meta,),
+        est=cost(0, 12 * QUARTER * width),
+    )
     return call(
-        functools.partial(gather_kernel, scaled),
-        (4,),
-        specs + [whole(p.shape) for p in pieces],
-        pl.BlockSpec((1, QUARTER, width), lambda i, m: (0, tok_block((m[0] & 3) ^ i), 0)),
-        sds((1, 4 * QUARTER, width), BF16),
-        (*extra, *pieces),
+        functools.partial(gather_kernel, scaled, False),
+        (1,),
+        [pl.BlockSpec(memory_space=pl.ANY)] + specs + [whole(p.shape) for p in pieces[3:]],
+        out(3),
+        result,
+        (part, *extra, *pieces[3:]),
         (meta,),
-        est=cost(0, 16 * QUARTER * width),
+        est=cost(0, 4 * QUARTER * width),
+        alias={1: 0},
     )
 
 
@@ -1123,71 +1203,72 @@
         ]
         return lax.ppermute(value, axes, pairs)
 
+    def plane(first, second, third):
+        values = (first, second, third)
+        return [send(value, 0, n + 1) for n, value in enumerate(values)]
+
+    def swap(values):
+        return [send(value, 1, 0) for value in values]
+
+    half = QUARTER // 2
+
+    def spread(own):
+        from_x = send(own, 0, 1)
+        from_y = send(own, 0, 2)
+        cut_x, cut_y = from_x[:half], from_y[half:]
+        return [own, from_x, from_y, send(cut_x, 0, 2), send(cut_y, 0, 1)]
+
     tensor_at = lax.axis_index("tensor")
     core = lax.axis_index("dp") & 1
     meta = (tensor_at + 4 * core).astype(jnp.int32).reshape(1)
     down_t = jnp.swapaxes(adapter_down, 1, 2)
     vec = vector_parameters
     length = inputs.shape[1]
-
-    one = core.astype(jnp.int32).reshape(1)
     ffn = (hidden_weight, hidden_output_weight, hidden_bias)
-    pack_x, pack_y, pack_d = fetch_packs(one, *ffn, attention_output_weight)
-    got_x = send(pack_x, 0, 1)
-    got_y = send(pack_y, 0, 2)
-    got_d = send(pack_d, 0, 3)
+
+    local_rows = attention_output_weight.shape[0] // 2
+    mine = lax.dynamic_slice_in_dim(attention_output_weight, core * local_rows, local_rows, 0)
+    xa, xb, ya, yb = fetch_packs(core.astype(jnp.int32).reshape(1), *ffn, attention_output_weight)
+    got_d = send(mine, 0, 3)
+    got_x, got_y = send(xa, 0, 1), send(ya, 0, 2)
 
     q, k, v, norm1, lora = qkv(
         meta, inputs, vec, query_key_value_weight, query_value_bias, down_t, adapter_up
     )
     probs, out_t, same, other = attend_fast(meta, q, k, v)
-    heads = [same, send(other, 0, 1), send(other, 0, 2), send(same, 0, 3)]
-    swap_x = send(got_x, 1, 0)
-    swap_y = send(got_y, 1, 0)
-    swap_d = send(got_d, 1, 0)
-    own_packs = pack(jnp.arange(4, dtype=jnp.int32), 4, *ffn)
+    heads = [same] + plane(other, other, same)
+    late_x, late_y = send(xb, 0, 1), send(yb, 0, 2)
+    swap_x, swap_y, swap_d = swap((got_x, got_y, got_d))
+    own = pack(*ffn)
     wof = project(
         meta, attention_output_weight, (got_x, swap_x, got_y, swap_y), (got_d, swap_d)
     )
-    packs = [own_packs, got_x, swap_x, got_y, swap_y]
-
-    gn_pair, mlp_pair, _ = mlp_fast(
-        False, meta, groups, counts, inputs, cotangent, vec, heads, wof, packs
-    )
+    entry = (groups, counts, inputs, cotangent, vec, heads, wof)
+    early = [(got_x, got_y), (swap_x, swap_y)]
+    gn, mlp, n2, low = mlp_call(meta, 3, entry, None, own, early, False)
+    late = [(late_x, late_y), tuple(swap((late_x, late_y)))]
+    gn_pair, mlp_pair = mlp_call(meta, 3, None, (n2, low, gn, mlp), None, late, True)
     gn_recv = send(gn_pair, 0, 3)
     mlp_recv = send(mlp_pair, 0, 3)
-    gn_own, mlp_own, resid = mlp_fast(
-        True, meta, groups, counts, inputs, cotangent, vec, heads, wof, packs
-    )
+    gn_own, mlp_own, resid = mlp_call(meta, 0, entry, None, own, early + late, True)
     grad_resid, g_own, g_x, g_y, g_d = resid_back(
         meta, groups, counts, gn_own, gn_recv, resid, cotangent, vec, wof
     )
-    pieces = [g_own, send(g_x, 0, 1), send(g_y, 0, 2), send(g_d, 0, 3)]
+    pieces = [g_own] + plane(g_x, g_y, g_d)
     out_own = (resid + mlp_own + mlp_recv.astype(F32) + vec[5]).astype(BF16)
-    half = QUARTER // 2
-
-    def spread(own):
-        from_x = send(own, 0, 1)
-        from_y = send(own, 0, 2)
-        cut_x, cut_y = from_x[:half], from_y[half:]
-        return [own, from_x, from_y, send(cut_x, 0, 2), send(cut_y, 0, 1)]
-
     out_all = spread(out_own)
 
     dq, dk, dv = attend_back_fast(meta, q, k, v, probs, out_t, pieces)
     gx, gy, gd, g1_own = input_back(
         meta, dq, dk, dv, query_key_value_weight, down_t, adapter_up
     )
-    g1 = [send(gx, 0, 1), send(gy, 0, 2), send(gd, 0, 3)]
+    g1 = plane(gx, gy, gd)
     total = adapter_grads(meta, groups, counts, dq, dv, adapter_up, norm1, lora)
-    sum_x = send(total, 0, 1)
-    sum_y = send(total, 0, 2)
-    sum_d = send(total, 0, 3)
+    sum_x, sum_y, sum_d = plane(total, total, total)
     total = (total + sum_x) + (sum_y + sum_d)
     step = 1
     while step < dp_size:
-        got = send(total, step, 0)
-        total = total + got
+        total = total + send(total, step, 0)
         step *= 2
     in_own = first_back(meta, g1_own, g1, inputs, grad_resid, vec)
     in_all = spread(in_own)

time: 212 us -> 195 us (0.920)
  Pallas kernels: 81.9 us -> 68.2 us
  waiting for transfers between devices: 89.5 us -> 80.7 us
  local copies, waits for them, and re-layouts: 1.58 us -> 4.83 us
  starting transfers between devices: 36.3 us -> 39.4 us
    pallas_call x15 -> x18, Pallas kernels: 81.9 us -> 68.2 us  [call(): pl.pallas_call(kernel, grid_spec=pltpu.PrefetchScalarGridSpec(num_scalar_...]
    ppermute x31 -> x35, waiting for transfers between devices: 89.5 us -> 80.7 us  [send(): return lax.ppermute(value, axes, pairs)]
    ppermute x31 -> x35, starting transfers between devices: 36.3 us -> 39.4 us  [send(): return lax.ppermute(value, axes, pairs)]
  transfers between devices with their start and end apart: 31 -> 35, of which waited for: 14 -> 15; matrix products, arithmetic and copies ran while one was open for 0% -> 1% of each run, Pallas kernels for 28% -> 30%
where the time goes in v1:
time: 195 us
  waiting for transfers between devices  80.7 us (41%)
  Pallas kernels  68.2 us (35%)
  starting transfers between devices  39.4 us (20%)
  local copies, waits for them, and re-layouts  4.83 us (2%)
    ppermute x35, waiting for transfers between devices, send(): return lax.ppermute(value, axes, pairs)  80.7 us
    pallas_call x18, Pallas kernels, call(): pl.pallas_call(kernel, grid_spec=pltpu.PrefetchScalarGridSpec(num_scalar_...  68.2 us
    ppermute x35, starting transfers between devices, send(): return lax.ppermute(value, axes, pairs)  39.4 us
  transfers between devices with their start and end apart: 35, of which 15 were waited for; matrix products, arithmetic and copies ran while one was open for 1% of the time, Pallas kernels for 30%

profile of v1, /device:TPU:0, one launch (start us, length us, event | category | flops | bytes accessed | tf_op | source)
XLA Modules:
  0.0 195.1 jit_solution(2326299751646755254)
XLA Ops:
  0.7 3.5 %shard_map.258 = (bf16[400,1024]{1,0:T(8,128)(2,1)}, bf16[272,1024]{1,0:T(8,128)(2,1)}, bf16[400,1024]{1,0:T(8,128)(2,1)}, bf16[272,1024]{1,0:T(8,128)(2,1)}) custom-call(s32[1]{0:T(128)} %bitcast.2.core_ref, bf16[1024,1024]{1,0:T(8,128)(2,1)} %wh_ref.1, bf16[1024,1024]{1,0:T(8,128)(2,1)} %wo_ref.1, f32[1,1024]{1,0:T(1,128)} %bitcast.12, ...), custom_call_target="tpu_custom_call" | custom-call | bytes 4456448 | tf_op jit(solution)/shard_map/pallas_call | solution.py:376
  4.2 3.0 %collective-permute-start.3 = (bf16[400,1024]{1,0:T(8,128)(2,1)}, bf16[400,1024]{1,0:T(8,128)(2,1)S(1)}, u32[]{:S(2)}, u32[]{:S(2)}) collective-permute-start(bf16[400,1024]{1,0:T(8,128)(2,1)} %get-tuple-element.61), channel_id=1, source_target_pairs={{0,1},{1,0},{2,3},{3,2},{4,5},{5,4},{6,7},{7,6},{8,9},{9,8},{10,11... | collective-permute-start | bytes 2457608 | tf_op jit(solution)/shard_map/ppermute | solution.py:1204
  7.1 1.5 collective-permute-start.5
  8.7 16.9 %collective-permute-done.3.refs_0_.refs_12_ = bf16[400,1024]{1,0:T(8,128)(2,1)S(1)} collective-permute-done((bf16[400,1024]{1,0:T(8,128)(2,1)}, bf16[400,1024]{1,0:T(8,128)(2,1)S(1)}, u32[]{:S(2)}, u32[]{:S(2)}) %collective-permute-start.3) | collective-permute-done | bytes 819232 | tf_op jit(solution)/shard_map/ppermute | solution.py:1204
  25.6 1.5 collective-permute-done.5.refs_2_.refs_13_
  27.0 1.7 constant_dynamic-slice_fusion
  28.7 1.7 collective-permute-start.7
  30.5 1.2 collective-permute-start.9
  31.7 0.5 collective-permute-start.10
  32.2 6.9 %collective-permute-done.7.refs_4_ = bf16[128,1024]{1,0:T(8,128)(2,1)} collective-permute-done((bf16[128,1024]{1,0:T(8,128)(2,1)}, bf16[128,1024]{1,0:T(8,128)(2,1)}, u32[]{:S(2)}, u32[]{:S(2)}) %collective-permute-start.7) | collective-permute-done | bytes 262176 | tf_op jit(solution)/shard_map/ppermute | solution.py:1204
  39.2 1.6 copy-done.2
  40.8 1.4 copy-done.15
  42.2 5.5 %shard_map.256 = (bf16[1024,256]{1,0:T(8,128)(2,1)S(1)}, bf16[1024,256]{1,0:T(8,128)(2,1)S(1)}, bf16[1024,256]{1,0:T(8,128)(2,1)S(1)}, bf16[1024,1024]{1,0:T(8,128)(2,1)S(1)}, bf16[1024,128]{1,0:T(8,128)(2,1)S(1)}) custom-call(s32[1]{0:T(128)} %bitcast.meta_ref.refs_0_, bf16[1,1024,1024]{2,1,0:T(8,128)(2,1)S(1)} %copy-done.2, f32[6,1024]{1,0:T(8,128)S(1)} %copy-done.6, ...), custom_call_target="tpu_custom_call" | custom-call | flops 1610612736 | bytes 7340032 | tf_op jit(solution)/shard_map/pallas_call | solution.py:376
  47.8 10.7 %shard_map.257 = (bf16[4,1024,1024]{2,1,0:T(8,128)(2,1)S(1)}, f32[256,1024]{1,0:T(8,128)S(1)}, bf16[512,256]{1,0:T(8,128)(2,1)S(1)}, bf16[512,256]{1,0:T(8,128)(2,1)S(1)}) custom-call(s32[1]{0:T(128)} %bitcast.meta_ref.refs_0_, bf16[1024,256]{1,0:T(8,128)(2,1)S(1)} %get-tuple-element.56.q_ref, bf16[1024,256]{1,0:T(8,128)(2,1)S(1)} %get-tuple-element.57.k_ref, ...), custom_call_target="tpu_custom_call" | custom-call | flops 2147483648 | bytes 11010048 | tf_op jit(solution)/shard_map/pallas_call | solution.py:376
  58.5 0.9 collective-permute-start
  59.3 1.5 collective-permute-start.1
  60.8 1.2 collective-permute-start.2
  62.0 0.5 collective-permute-start.12
  62.5 1.2 shard_map.260.refs_11_
  64.4 1.2 shard_map.259.refs_10_.wof_ref
  65.7 2.0 %collective-permute-done.refs_7_ = bf16[512,256]{1,0:T(8,128)(2,1)S(1)} collective-permute-done((bf16[512,256]{1,0:T(8,128)(2,1)S(1)}, bf16[512,256]{1,0:T(8,128)(2,1)S(1)}, u32[]{:S(2)}, u32[]{:S(2)}) %collective-permute-start) | collective-permute-done | bytes 262176 | tf_op jit(solution)/shard_map/ppermute | solution.py:1204
  67.7 4.7 %collective-permute-done.1.refs_8_ = bf16[512,256]{1,0:T(8,128)(2,1)S(1)} collective-permute-done((bf16[512,256]{1,0:T(8,128)(2,1)S(1)}, bf16[512,256]{1,0:T(8,128)(2,1)S(1)}, u32[]{:S(2)}, u32[]{:S(2)}) %collective-permute-start.1) | collective-permute-done | bytes 262176 | tf_op jit(solution)/shard_map/ppermute | solution.py:1204
  72.4 1.4 collective-permute-done.2.refs_9_
  73.8 8.5 %shard_map.262 = (f32[256,1024]{1,0:T(8,128)S(1)}, f32[256,1024]{1,0:T(8,128)S(1)}, bf16[256,1024]{1,0:T(8,128)(2,1)S(1)}, bf16[256,1024]{1,0:T(8,128)(2,1)S(1)}) custom-call(s32[1]{0:T(128)} %bitcast.meta_ref.refs_0_, s32[1]{0:T(128)S(6)} %copy.33.refs_1_.groups_ref, s32[8]{0:T(128)S(1)} %copy-done.14, bf16[1,1024,1024]{2,1,0:T(8,128)(2,1)S(1)} %copy-done.3, ...), custom_call_target="tpu_custom_call" | custom-call | flops 3758096384 | bytes 12582912 | tf_op jit(solution)/shard_map/pallas_call | solution.py:376
  82.4 3.1 %shard_map.263 = (bf16[256,1024]{1,0:T(8,128)(2,1)S(1)}, bf16[256,1024]{1,0:T(8,128)(2,1)S(1)}) custom-call(s32[1]{0:T(128)} %bitcast.meta_ref.refs_0_, bf16[256,1024]{1,0:T(8,128)(2,1)S(1)} %get-tuple-element.67.refs_1_, bf16[256,1024]{1,0:T(8,128)(2,1)S(1)} %get-tuple-element.68.refs_2_, f32[256,1024]{1,0:T(8,128)S(1)} %get-tuple-element.69.refs_3_, ...), custom_call_target="tpu_custom_call" | custom-call | flops 1073741824 | bytes 8388608 | tf_op jit(solution)/shard_map/pallas_call | solution.py:376
  85.4 1.8 collective-permute-start.18
  87.3 11.0 %shard_map.261 = (f32[256,1024]{1,0:T(8,128)S(1)}, f32[256,1024]{1,0:T(8,128)S(1)}, f32[256,1024]{1,0:T(8,128)S(1)}) custom-call(s32[1]{0:T(128)} %bitcast.meta_ref.refs_0_, s32[1]{0:T(128)S(6)} %copy.33.refs_1_.groups_ref, s32[8]{0:T(128)S(1)} %copy-done.14, bf16[1,1024,1024]{2,1,0:T(8,128)(2,1)S(1)} %copy-done.3, bf16[1,1024,1024]{2,1,0:T(8,128)(2,1)S(1)} %copy-done.4, ...), custom_call_target="tpu_custom_call" | custom-call | flops 4831838208 | bytes 14680064 | tf_op jit(solution)/shard_map/pallas_call | solution.py:376
  98.2 1.6 collective-permute-done.18.recv_ref
  99.8 1.9 shard_map.266
  101.8 0.9 collective-permute-start.19
  102.6 1.2 collective-permute-start.20
  103.9 1.4 collective-permute-start.21
  105.3 1.5 collective-permute-start.13
  106.8 1.4 collective-permute-done.19.gx_ref
  108.2 13.0 %collective-permute-done.20.gy_ref = bf16[256,256]{1,0:T(8,128)(2,1)S(1)} collective-permute-done((bf16[256,256]{1,0:T(8,128)(2,1)S(1)}, bf16[256,256]{1,0:T(8,128)(2,1)S(1)}, u32[]{:S(2)}, u32[]{:S(2)}) %collective-permute-start.20) | collective-permute-done | bytes 131104 | tf_op jit(solution)/shard_map/ppermute | solution.py:1204
  121.2 8.3 %shard_map.267 = (bf16[1024,256]{1,0:T(8,128)(2,1)S(1)}, bf16[1024,256]{1,0:T(8,128)(2,1)S(1)}, bf16[1024,256]{1,0:T(8,128)(2,1)S(1)}) custom-call(s32[1]{0:T(128)} %bitcast.meta_ref.refs_0_, bf16[1024,256]{1,0:T(8,128)(2,1)S(1)} %get-tuple-element.56.q_ref, bf16[1024,256]{1,0:T(8,128)(2,1)S(1)} %get-tuple-element.57.k_ref, ...), custom_call_target="tpu_custom_call" | custom-call | flops 4294967296 | bytes 12582912 | tf_op jit(solution)/shard_map/pallas_call | solution.py:376
  129.5 3.6 %shard_map.269 = (bf16[256,1024]{1,0:T(8,128)(2,1)S(1)}, bf16[256,1024]{1,0:T(8,128)(2,1)S(1)}, bf16[256,1024]{1,0:T(8,128)(2,1)S(1)}, f32[256,1024]{1,0:T(8,128)S(1)}) custom-call(s32[1]{0:T(128)} %bitcast.meta_ref.refs_0_, bf16[1024,256]{1,0:T(8,128)(2,1)S(1)} %get-tuple-element.80.dq_ref, bf16[1024,256]{1,0:T(8,128)(2,1)S(1)} %get-tuple-element.84.dk_ref, ...), custom_call_target="tpu_custom_call" | custom-call | flops 1610612736 | bytes 9437184 | tf_op jit(solution)/shard_map/pallas_call | solution.py:376
  133.1 0.7 collective-permute-start.28
  133.8 1.4 collective-permute-start.29
  135.2 1.5 collective-permute-start.30
  136.7 2.5 %shard_map.268 = f32[24,1024]{1,0:T(8,128)S(1)} custom-call(s32[1]{0:T(128)} %bitcast.meta_ref.refs_0_, s32[1]{0:T(128)S(6)} %copy.33.refs_1_.groups_ref, s32[8]{0:T(128)S(1)} %copy-done.14, bf16[1024,256]{1,0:T(8,128)(2,1)S(1)} %get-tuple-element.80.dq_ref, bf16[1024,256]{1,0:T(8,128)(2,1)S(1)} %get-tuple-element.81.dv_ref, f32[2,4,1024]{2,1,0:T(4,128)S(1)} %copy-done.7, ...), custom_call_target="tpu_custom_call" | custom-call | flops 268435456 | bytes 3145728 | tf_op jit(solution)/shard_map/pallas_call | solution.py:376
  139.2 1.0 collective-permute-start.23
  140.5 1.1 collective-permute-start.14
  141.6 6.4 %collective-permute-done.28.a_ref = bf16[256,1024]{1,0:T(8,128)(2,1)S(1)} collective-permute-done((bf16[256,1024]{1,0:T(8,128)(2,1)S(1)}, bf16[256,1024]{1,0:T(8,128)(2,1)S(1)}, u32[]{:S(2)}, u32[]{:S(2)}) %collective-permute-start.28) | collective-permute-done | bytes 524320 | tf_op jit(solution)/shard_map/ppermute | solution.py:1204
  148.0 1.0 collective-permute-start.15
  149.0 8.5 %collective-permute-done.30.c_ref = bf16[256,1024]{1,0:T(8,128)(2,1)S(1)} collective-permute-done((bf16[256,1024]{1,0:T(8,128)(2,1)S(1)}, bf16[256,1024]{1,0:T(8,128)(2,1)S(1)}, u32[]{:S(2)}, u32[]{:S(2)}) %collective-permute-start.30) | collective-permute-done | bytes 524320 | tf_op jit(solution)/shard_map/ppermute | solution.py:1204
  157.5 0.9 shard_map.270.refs_1_
  158.4 1.7 collective-permute-start.31
  160.3 1.7 collective-permute-start.24
  162.0 8.9 %collective-permute-done.24 = f32[24,1024]{1,0:T(8,128)S(1)} collective-permute-done((f32[24,1024]{1,0:T(8,128)S(1)}, f32[24,1024]{1,0:T(8,128)S(1)}, u32[]{:S(2)}, u32[]{:S(2)}) %collective-permute-start.24) | collective-permute-done | bytes 98336 | tf_op jit(solution)/shard_map/ppermute | solution.py:1204
  170.9 1.6 collective-permute-start.22
  172.5 3.0 %collective-permute-done.22 = f32[24,1024]{1,0:T(8,128)S(1)} collective-permute-done((f32[24,1024]{1,0:T(8,128)S(1)}, f32[24,1024]{1,0:T(8,128)S(1)}, u32[]{:S(2)}, u32[]{:S(2)}) %collective-permute-start.22) | collective-permute-done | bytes 98336 | tf_op jit(solution)/shard_map/ppermute | solution.py:1204
  175.6 1.4 collective-permute-start.16
  177.6 1.9 collective-permute-start.33
  179.5 0.5 collective-permute-start.34
  180.1 1.6 collective-permute-start.26
  181.7 3.0 %collective-permute-done.26 = f32[24,1024]{1,0:T(8,128)S(1)} collective-permute-done((f32[24,1024]{1,0:T(8,128)S(1)}, f32[24,1024]{1,0:T(8,128)S(1)}, u32[]{:S(2)}, u32[]{:S(2)}) %collective-permute-start.26) | collective-permute-done | bytes 98336 | tf_op jit(solution)/shard_map/ppermute | solution.py:1204
  184.8 2.6 %collective-permute-start.27 = (f32[24,1024]{1,0:T(8,128)S(1)}, f32[24,1024]{1,0:T(8,128)S(1)}, u32[]{:S(2)}, u32[]{:S(2)}) collective-permute-start(f32[24,1024]{1,0:T(8,128)S(1)} %add.51), channel_id=1, source_target_pairs={{0,16},{1,17},{2,18},{3,19},{4,20},{5,21},{6,22},{7,23},{8,24},{9,... | collective-permute-start | bytes 294920 | tf_op jit(solution)/shard_map/ppermute | solution.py:1204
  187.4 1.7 shard_map.264.refs_0_
  189.1 1.3 collective-permute-done.27
  190.4 0.8 shard_map.273
  191.2 0.8 shard_map.265
  192.1 2.0 %shard_map.271.refs_0_ = bf16[1,1024,1024]{2,1,0:T(8,128)(2,1)} custom-call(s32[1]{0:T(128)} %bitcast.meta_ref.refs_0_, f32[24,1024]{1,0:T(8,128)S(1)} %add.52.refs_0_.refs_1_.total_ref, bf16[256,1024]{1,0:T(8,128)(2,1)S(1)} %shard_map.270.refs_1_, bf16[256,1024]{1,0:T(8,128)(2,1)S(1)} %collective-permute-done.31.refs_2_, ...), custom_call_target="tpu_custom_call" | custom-call | bytes 3145728 | tf_op jit(solution)/shard_map/pallas_call | solution.py:376
  194.1 1.0 shard_map.272
  (71 shorter events, 1.3 us)
Async XLA Ops:
  0.7 38.5 %copy-start.6 = (f32[6,1024]{1,0:T(8,128)S(1)}, f32[6,1024]{1,0:T(8,128)}, u32[]{:S(2)}) copy-start(f32[6,1024]{1,0:T(8,128)} %vec_ref.5) | copy-start | bytes 73732
  0.7 38.5 %copy-start.7 = (f32[2,4,1024]{2,1,0:T(4,128)S(1)}, f32[2,4,1024]{2,1,0:T(4,128)}, u32[]{:S(2)}) copy-start(f32[2,4,1024]{2,1,0:T(4,128)} %u_ref.1) | copy-start | bytes 98308
  0.7 38.5 %copy-start.9 = (f32[2,1024,4]{1,2,0:T(4,128)S(1)}, f32[2,1024,4]{1,2,0:T(4,128)}, u32[]{:S(2)}) copy-start(f32[2,1024,4]{1,2,0:T(4,128)} %param.28) | copy-start | bytes 98308
  0.7 38.5 %copy-start.17 = (f32[2,256]{1,0:T(2,128)S(1)}, f32[2,256]{1,0:T(2,128)}, u32[]{:S(2)}) copy-start(f32[2,256]{1,0:T(2,128)} %qvb_ref.1) | copy-start | bytes 6148
  4.2 21.4 %collective-permute-start.3 = (bf16[400,1024]{1,0:T(8,128)(2,1)}, bf16[400,1024]{1,0:T(8,128)(2,1)S(1)}, u32[]{:S(2)}, u32[]{:S(2)}) collective-permute-start(bf16[400,1024]{1,0:T(8,128)(2,1)} %get-tuple-element.61), channel_id=1, source_target_pairs={{0,1},{1,0},{2,3},{3,2},{4,5},{5,4},{6,7},{7,6},{8,9},{9,8},{10,11... | collective-permute-start | bytes 2457608 | tf_op jit(solution)/shard_map/ppermute | solution.py:1204
  7.1 19.9 %collective-permute-start.5 = (bf16[400,1024]{1,0:T(8,128)(2,1)}, bf16[400,1024]{1,0:T(8,128)(2,1)S(1)}, u32[]{:S(2)}, u32[]{:S(2)}) collective-permute-start(bf16[400,1024]{1,0:T(8,128)(2,1)} %get-tuple-element.62), channel_id=1, source_target_pairs={{0,2},{1,3},{2,0},{3,1},{4,6},{5,7},{6,4},{7,5},{8,10},{9,11},{10,... | collective-permute-start | bytes 2457608 | tf_op jit(solution)/shard_map/ppermute | solution.py:1204
  25.6 36.4 %collective-permute-start.4 = (bf16[400,1024]{1,0:T(8,128)(2,1)S(1)}, bf16[400,1024]{1,0:T(8,128)(2,1)S(1)}, u32[]{:S(2)}, u32[]{:S(2)}) collective-permute-start(bf16[400,1024]{1,0:T(8,128)(2,1)S(1)} %collective-permute-done.3.refs_0_.refs_12_), channel_id=1, source_target_pairs={{0,4},{1,5},{2,6},{3,7},{4,0},{5,1},{6,2},{7,3},{8,12},{9,13},{10,... | collective-permute-start | bytes 2457608 | tf_op jit(solution)/shard_map/ppermute | solution.py:1204
  27.0 35.0 %collective-permute-start.6 = (bf16[400,1024]{1,0:T(8,128)(2,1)S(1)}, bf16[400,1024]{1,0:T(8,128)(2,1)S(1)}, u32[]{:S(2)}, u32[]{:S(2)}) collective-permute-start(bf16[400,1024]{1,0:T(8,128)(2,1)S(1)} %collective-permute-done.5.refs_2_.refs_13_), channel_id=1, source_target_pairs={{0,4},{1,5},{2,6},{3,7},{4,0},{5,1},{6,2},{7,3},{8,12},{9,13},{10,... | collective-permute-start | bytes 2457608 | tf_op jit(solution)/shard_map/ppermute | solution.py:1204
  28.7 10.4 %collective-permute-start.7 = (bf16[128,1024]{1,0:T(8,128)(2,1)}, bf16[128,1024]{1,0:T(8,128)(2,1)}, u32[]{:S(2)}, u32[]{:S(2)}) collective-permute-start(bf16[128,1024]{1,0:T(8,128)(2,1)} %constant_dynamic-slice_fusion), channel_id=1, source_target_pairs={{0,3},{1,2},{2,1},{3,0},{4,7},{5,6},{6,5},{7,4},{8,11},{9,10},{10,... | collective-permute-start | bytes 786440 | tf_op jit(solution)/shard_map/ppermute | solution.py:1204
  30.5 28.9 %collective-permute-start.9 = (bf16[272,1024]{1,0:T(8,128)(2,1)}, bf16[272,1024]{1,0:T(8,128)(2,1)}, u32[]{:S(2)}, u32[]{:S(2)}) collective-permute-start(bf16[272,1024]{1,0:T(8,128)(2,1)} %get-tuple-element.63), channel_id=1, source_target_pairs={{0,1},{1,0},{2,3},{3,2},{4,5},{5,4},{6,7},{7,6},{8,9},{9,8},{10,11... | collective-permute-start | bytes 1671176 | tf_op jit(solution)/shard_map/ppermute | solution.py:1204
  31.7 29.1 %collective-permute-start.10 = (bf16[272,1024]{1,0:T(8,128)(2,1)}, bf16[272,1024]{1,0:T(8,128)(2,1)}, u32[]{:S(2)}, u32[]{:S(2)}) collective-permute-start(bf16[272,1024]{1,0:T(8,128)(2,1)} %get-tuple-element.64), channel_id=1, source_target_pairs={{0,2},{1,3},{2,0},{3,1},{4,6},{5,7},{6,4},{7,5},{8,10},{9,11},{10,... | collective-permute-start | bytes 1671176 | tf_op jit(solution)/shard_map/ppermute | solution.py:1204
  39.2 19.3 %collective-permute-start.8 = (bf16[128,1024]{1,0:T(8,128)(2,1)}, bf16[128,1024]{1,0:T(8,128)(2,1)S(1)}, u32[]{:S(2)}, u32[]{:S(2)}) collective-permute-start(bf16[128,1024]{1,0:T(8,128)(2,1)} %collective-permute-done.7.refs_4_), channel_id=1, source_target_pairs={{0,4},{1,5},{2,6},{3,7},{4,0},{5,1},{6,2},{7,3},{8,12},{9,13},{10,... | collective-permute-start | bytes 786440 | tf_op jit(solution)/shard_map/ppermute | solution.py:1204
  39.2 1.6 copy-start.2
  40.8 1.4 copy-start.15
  47.7 14.8 %copy-start = (bf16[1024,1024]{1,0:T(8,128)(2,1)S(1)}, bf16[1024,1024]{1,0:T(8,128)(2,1)}, u32[]{:S(2)}) copy-start(bf16[1024,1024]{1,0:T(8,128)(2,1)} %wh_ref.1) | copy-start | bytes 6291460
  47.7 14.8 %copy-start.1 = (bf16[1024,1024]{1,0:T(8,128)(2,1)S(1)}, bf16[1024,1024]{1,0:T(8,128)(2,1)}, u32[]{:S(2)}) copy-start(bf16[1024,1024]{1,0:T(8,128)(2,1)} %wo_ref.1) | copy-start | bytes 6291460
  47.7 14.8 %copy-start.8 = (f32[1024]{0:T(1024)S(1)}, f32[1024]{0:T(1024)}, u32[]{:S(2)}) copy-start(f32[1024]{0:T(1024)} %param.23) | copy-start | bytes 12292
  58.5 9.2 %collective-permute-start = (bf16[512,256]{1,0:T(8,128)(2,1)S(1)}, bf16[512,256]{1,0:T(8,128)(2,1)S(1)}, u32[]{:S(2)}, u32[]{:S(2)}) collective-permute-start(bf16[512,256]{1,0:T(8,128)(2,1)S(1)} %get-tuple-element.60), channel_id=1, source_target_pairs={{0,1},{1,0},{2,3},{3,2},{4,5},{5,4},{6,7},{7,6},{8,9},{9,8},{10,11... | collective-permute-start | bytes 786440 | tf_op jit(solution)/shard_map/ppermute | solution.py:1204
  59.3 13.1 %collective-permute-start.1 = (bf16[512,256]{1,0:T(8,128)(2,1)S(1)}, bf16[512,256]{1,0:T(8,128)(2,1)S(1)}, u32[]{:S(2)}, u32[]{:S(2)}) collective-permute-start(bf16[512,256]{1,0:T(8,128)(2,1)S(1)} %get-tuple-element.60), channel_id=1, source_target_pairs={{0,2},{1,3},{2,0},{3,1},{4,6},{5,7},{6,4},{7,5},{8,10},{9,11},{10,... | collective-permute-start | bytes 786440 | tf_op jit(solution)/shard_map/ppermute | solution.py:1204
  60.8 3.5 %copy-start.5 = (bf16[256,1024]{1,0:T(8,128)(2,1)S(1)}, bf16[256,1024]{1,0:T(8,128)(2,1)}, u32[]{:S(2)}) copy-start(bf16[256,1024]{1,0:T(8,128)(2,1)} %own_ref.1) | copy-start | bytes 1572868
  60.8 13.0 %collective-permute-start.2 = (bf16[512,256]{1,0:T(8,128)(2,1)S(1)}, bf16[512,256]{1,0:T(8,128)(2,1)S(1)}, u32[]{:S(2)}, u32[]{:S(2)}) collective-permute-start(bf16[512,256]{1,0:T(8,128)(2,1)S(1)} %get-tuple-element.59.refs_6_), channel_id=1, source_target_pairs={{0,3},{1,2},{2,1},{3,0},{4,7},{5,6},{6,5},{7,4},{8,11},{9,10},{10,... | collective-permute-start | bytes 786440 | tf_op jit(solution)/shard_map/ppermute | solution.py:1204
  62.0 20.3 %collective-permute-start.11 = (bf16[272,1024]{1,0:T(8,128)(2,1)}, bf16[272,1024]{1,0:T(8,128)(2,1)S(1)}, u32[]{:S(2)}, u32[]{:S(2)}) collective-permute-start(bf16[272,1024]{1,0:T(8,128)(2,1)} %collective-permute-done.9.refs_16_.refs_5_), channel_id=1, source_target_pairs={{0,4},{1,5},{2,6},{3,7},{4,0},{5,1},{6,2},{7,3},{8,12},{9,13},{10,... | collective-permute-start | bytes 1671176 | tf_op jit(solution)/shard_map/ppermute | solution.py:1204
  62.0 20.3 %collective-permute-start.12 = (bf16[272,1024]{1,0:T(8,128)(2,1)}, bf16[272,1024]{1,0:T(8,128)(2,1)S(1)}, u32[]{:S(2)}, u32[]{:S(2)}) collective-permute-start(bf16[272,1024]{1,0:T(8,128)(2,1)} %collective-permute-done.10.refs_17_.refs_6_), channel_id=1, source_target_pairs={{0,4},{1,5},{2,6},{3,7},{4,0},{5,1},{6,2},{7,3},{8,12},{9,13},{10,... | collective-permute-start | bytes 1671176 | tf_op jit(solution)/shard_map/ppermute | solution.py:1204
  64.4 9.4 %copy-start.3 = (bf16[1,1024,1024]{2,1,0:T(8,128)(2,1)S(1)}, bf16[1,1024,1024]{2,1,0:T(8,128)(2,1)}, u32[]{:S(2)}) copy-start(bf16[1,1024,1024]{2,1,0:T(8,128)(2,1)} %x_ref.3) | copy-start | bytes 6291460
  64.4 9.4 %copy-start.4 = (bf16[1,1024,1024]{2,1,0:T(8,128)(2,1)S(1)}, bf16[1,1024,1024]{2,1,0:T(8,128)(2,1)}, u32[]{:S(2)}) copy-start(bf16[1,1024,1024]{2,1,0:T(8,128)(2,1)} %cot_ref.1) | copy-start | bytes 6291460
  64.4 9.4 %copy-start.14 = (s32[8]{0:T(128)S(1)}, s32[8]{0:T(128)}, u32[]{:S(2)}) copy-start(s32[8]{0:T(128)} %counts_ref.3) | copy-start | bytes 100
  85.4 14.4 %collective-permute-start.18 = (bf16[256,1024]{1,0:T(8,128)(2,1)S(1)}, bf16[256,1024]{1,0:T(8,128)(2,1)S(1)}, u32[]{:S(2)}, u32[]{:S(2)}) collective-permute-start(bf16[256,1024]{1,0:T(8,128)(2,1)S(1)} %get-tuple-element.75), channel_id=1, source_target_pairs={{0,3},{1,2},{2,1},{3,0},{4,7},{5,6},{6,5},{7,4},{8,11},{9,10},{10,... | collective-permute-start | bytes 1572872 | tf_op jit(solution)/shard_map/ppermute | solution.py:1204
  101.8 6.4 %collective-permute-start.19 = (bf16[256,256]{1,0:T(8,128)(2,1)S(1)}, bf16[256,256]{1,0:T(8,128)(2,1)S(1)}, u32[]{:S(2)}, u32[]{:S(2)}) collective-permute-start(bf16[256,256]{1,0:T(8,128)(2,1)S(1)} %get-tuple-element.77), channel_id=1, source_target_pairs={{0,1},{1,0},{2,3},{3,2},{4,5},{5,4},{6,7},{7,6},{8,9},{9,8},{10,11... | collective-permute-start | bytes 393224 | tf_op jit(solution)/shard_map/ppermute | solution.py:1204
  102.6 18.5 %collective-permute-start.20 = (bf16[256,256]{1,0:T(8,128)(2,1)S(1)}, bf16[256,256]{1,0:T(8,128)(2,1)S(1)}, u32[]{:S(2)}, u32[]{:S(2)}) collective-permute-start(bf16[256,256]{1,0:T(8,128)(2,1)S(1)} %get-tuple-element.78), channel_id=1, source_target_pairs={{0,2},{1,3},{2,0},{3,1},{4,6},{5,7},{6,4},{7,5},{8,10},{9,11},{10,... | collective-permute-start | bytes 393224 | tf_op jit(solution)/shard_map/ppermute | solution.py:1204
  103.9 17.3 %collective-permute-start.21 = (bf16[256,256]{1,0:T(8,128)(2,1)S(1)}, bf16[256,256]{1,0:T(8,128)(2,1)S(1)}, u32[]{:S(2)}, u32[]{:S(2)}) collective-permute-start(bf16[256,256]{1,0:T(8,128)(2,1)S(1)} %get-tuple-element.79), channel_id=1, source_target_pairs={{0,3},{1,2},{2,1},{3,0},{4,7},{5,6},{6,5},{7,4},{8,11},{9,10},{10,... | collective-permute-start | bytes 393224 | tf_op jit(solution)/shard_map/ppermute | solution.py:1204
  105.3 34.9 %collective-permute-start.13 = (bf16[256,1024]{1,0:T(8,128)(2,1)S(1)}, bf16[256,1024]{1,0:T(8,128)(2,1)S(1)}, u32[]{:S(2)}, u32[]{:S(2)}) collective-permute-start(bf16[256,1024]{1,0:T(8,128)(2,1)S(1)} %get-tuple-element.71), channel_id=1, source_target_pairs={{0,3},{1,2},{2,1},{3,0},{4,7},{5,6},{6,5},{7,4},{8,11},{9,10},{10,... | collective-permute-start | bytes 1572872 | tf_op jit(solution)/shard_map/ppermute | solution.py:1204
  121.2 8.3 %copy-start.16 = (bf16[3,1024,256]{2,1,0:T(8,128)(2,1)S(1)}, bf16[3,1024,256]{2,1,0:T(8,128)(2,1)}, u32[]{:S(2)}) copy-start(bf16[3,1024,256]{2,1,0:T(8,128)(2,1)} %w_ref.3) | copy-start | bytes 4718596
  133.1 14.9 %collective-permute-start.28 = (bf16[256,1024]{1,0:T(8,128)(2,1)S(1)}, bf16[256,1024]{1,0:T(8,128)(2,1)S(1)}, u32[]{:S(2)}, u32[]{:S(2)}) collective-permute-start(bf16[256,1024]{1,0:T(8,128)(2,1)S(1)} %get-tuple-element.86), channel_id=1, source_target_pairs={{0,1},{1,0},{2,3},{3,2},{4,5},{5,4},{6,7},{7,6},{8,9},{9,8},{10,11... | collective-permute-start | bytes 1572872 | tf_op jit(solution)/shard_map/ppermute | solution.py:1204
  133.8 15.1 %collective-permute-start.29 = (bf16[256,1024]{1,0:T(8,128)(2,1)S(1)}, bf16[256,1024]{1,0:T(8,128)(2,1)S(1)}, u32[]{:S(2)}, u32[]{:S(2)}) collective-permute-start(bf16[256,1024]{1,0:T(8,128)(2,1)S(1)} %get-tuple-element.87), channel_id=1, source_target_pairs={{0,2},{1,3},{2,0},{3,1},{4,6},{5,7},{6,4},{7,5},{8,10},{9,11},{10,... | collective-permute-start | bytes 1572872 | tf_op jit(solution)/shard_map/ppermute | solution.py:1204
  135.2 22.3 %collective-permute-start.30 = (bf16[256,1024]{1,0:T(8,128)(2,1)S(1)}, bf16[256,1024]{1,0:T(8,128)(2,1)S(1)}, u32[]{:S(2)}, u32[]{:S(2)}) collective-permute-start(bf16[256,1024]{1,0:T(8,128)(2,1)S(1)} %get-tuple-element.88), channel_id=1, source_target_pairs={{0,3},{1,2},{2,1},{3,0},{4,7},{5,6},{6,5},{7,4},{8,11},{9,10},{10,... | collective-permute-start | bytes 1572872 | tf_op jit(solution)/shard_map/ppermute | solution.py:1204
  139.2 21.1 %collective-permute-start.23 = (f32[24,1024]{1,0:T(8,128)S(1)}, f32[24,1024]{1,0:T(8,128)S(1)}, u32[]{:S(2)}, u32[]{:S(2)}) collective-permute-start(f32[24,1024]{1,0:T(8,128)S(1)} %shard_map.268), channel_id=1, source_target_pairs={{0,2},{1,3},{2,0},{3,1},{4,6},{5,7},{6,4},{7,5},{8,10},{9,11},{10,... | collective-permute-start | bytes 294920 | tf_op jit(solution)/shard_map/ppermute | solution.py:1204
  140.5 35.1 %collective-permute-start.14 = (bf16[256,1024]{1,0:T(8,128)(2,1)S(1)}, bf16[256,1024]{1,0:T(8,128)(2,1)S(1)}, u32[]{:S(2)}, u32[]{:S(2)}) collective-permute-start(bf16[256,1024]{1,0:T(8,128)(2,1)S(1)} %add_convert_fusion.refs_0_), channel_id=1, source_target_pairs={{0,1},{1,0},{2,3},{3,2},{4,5},{5,4},{6,7},{7,6},{8,9},{9,8},{10,11... | collective-permute-start | bytes 1572872 | tf_op jit(solution)/shard_map/ppermute | solution.py:1204
  148.0 29.1 %collective-permute-start.15 = (bf16[256,1024]{1,0:T(8,128)(2,1)S(1)}, bf16[256,1024]{1,0:T(8,128)(2,1)S(1)}, u32[]{:S(2)}, u32[]{:S(2)}) collective-permute-start(bf16[256,1024]{1,0:T(8,128)(2,1)S(1)} %add_convert_fusion.refs_0_), channel_id=1, source_target_pairs={{0,2},{1,3},{2,0},{3,1},{4,6},{5,7},{6,4},{7,5},{8,10},{9,11},{10,... | collective-permute-start | bytes 1572872 | tf_op jit(solution)/shard_map/ppermute | solution.py:1204
  158.4 19.2 %collective-permute-start.31 = (bf16[256,1024]{1,0:T(8,128)(2,1)S(1)}, bf16[256,1024]{1,0:T(8,128)(2,1)S(1)}, u32[]{:S(2)}, u32[]{:S(2)}) collective-permute-start(bf16[256,1024]{1,0:T(8,128)(2,1)S(1)} %shard_map.270.refs_1_), channel_id=1, source_target_pairs={{0,1},{1,0},{2,3},{3,2},{4,5},{5,4},{6,7},{7,6},{8,9},{9,8},{10,11... | collective-permute-start | bytes 1572872 | tf_op jit(solution)/shard_map/ppermute | solution.py:1204
  160.1 19.4 %collective-permute-start.32 = (bf16[256,1024]{1,0:T(8,128)(2,1)S(1)}, bf16[256,1024]{1,0:T(8,128)(2,1)S(1)}, u32[]{:S(2)}, u32[]{:S(2)}) collective-permute-start(bf16[256,1024]{1,0:T(8,128)(2,1)S(1)} %shard_map.270.refs_1_), channel_id=1, source_target_pairs={{0,2},{1,3},{2,0},{3,1},{4,6},{5,7},{6,4},{7,5},{8,10},{9,11},{10,... | collective-permute-start | bytes 1572872 | tf_op jit(solution)/shard_map/ppermute | solution.py:1204
  160.3 10.6 %collective-permute-start.24 = (f32[24,1024]{1,0:T(8,128)S(1)}, f32[24,1024]{1,0:T(8,128)S(1)}, u32[]{:S(2)}, u32[]{:S(2)}) collective-permute-start(f32[24,1024]{1,0:T(8,128)S(1)} %shard_map.268), channel_id=1, source_target_pairs={{0,3},{1,2},{2,1},{3,0},{4,7},{5,6},{6,5},{7,4},{8,11},{9,10},{10,... | collective-permute-start | bytes 294920 | tf_op jit(solution)/shard_map/ppermute | solution.py:1204
  170.9 4.6 %collective-permute-start.22 = (f32[24,1024]{1,0:T(8,128)S(1)}, f32[24,1024]{1,0:T(8,128)S(1)}, u32[]{:S(2)}, u32[]{:S(2)}) collective-permute-start(f32[24,1024]{1,0:T(8,128)S(1)} %shard_map.268), channel_id=1, source_target_pairs={{0,1},{1,0},{2,3},{3,2},{4,5},{5,4},{6,7},{7,6},{8,9},{9,8},{10,11... | collective-permute-start | bytes 294920 | tf_op jit(solution)/shard_map/ppermute | solution.py:1204
  175.5 4.5 %collective-permute-start.25 = (f32[24,1024]{1,0:T(8,128)S(1)}, f32[24,1024]{1,0:T(8,128)S(1)}, u32[]{:S(2)}, u32[]{:S(2)}) collective-permute-start(f32[24,1024]{1,0:T(8,128)S(1)} %add_add_fusion), channel_id=1, source_target_pairs={{0,4},{1,5},{2,6},{3,7},{4,0},{5,1},{6,2},{7,3},{8,12},{9,13},{10,... | collective-permute-start | bytes 294920 | tf_op jit(solution)/shard_map/ppermute | solution.py:1204
  175.6 15.6 %collective-permute-start.16 = (bf16[128,1024]{1,0:T(8,128)(2,1)S(1)}, bf16[128,1024]{1,0:T(8,128)(2,1)S(1)}, u32[]{:S(2)}, u32[]{:S(2)}) collective-permute-start(bf16[128,1024]{1,0:T(8,128)(2,1)S(1)} %slice.20), channel_id=1, source_target_pairs={{0,2},{1,3},{2,0},{3,1},{4,6},{5,7},{6,4},{7,5},{8,10},{9,11},{10,... | collective-permute-start | bytes 786440 | tf_op jit(solution)/shard_map/ppermute | solution.py:1204
  177.1 14.1 %collective-permute-start.17 = (bf16[128,1024]{1,0:T(8,128)(2,1)S(1)}, bf16[128,1024]{1,0:T(8,128)(2,1)S(1)}, u32[]{:S(2)}, u32[]{:S(2)}) collective-permute-start(bf16[128,1024]{1,0:T(8,128)(2,1)S(1)} %slice.21), channel_id=1, source_target_pairs={{0,1},{1,0},{2,3},{3,2},{4,5},{5,4},{6,7},{7,6},{8,9},{9,8},{10,11... | collective-permute-start | bytes 786440 | tf_op jit(solution)/shard_map/ppermute | solution.py:1204
  177.6 16.5 %collective-permute-start.33 = (bf16[128,1024]{1,0:T(8,128)(2,1)S(1)}, bf16[128,1024]{1,0:T(8,128)(2,1)S(1)}, u32[]{:S(2)}, u32[]{:S(2)}) collective-permute-start(bf16[128,1024]{1,0:T(8,128)(2,1)S(1)} %slice.22), channel_id=1, source_target_pairs={{0,2},{1,3},{2,0},{3,1},{4,6},{5,7},{6,4},{7,5},{8,10},{9,11},{10,... | collective-permute-start | bytes 786440 | tf_op jit(solution)/shard_map/ppermute | solution.py:1204
  179.5 14.6 %collective-permute-start.34 = (bf16[128,1024]{1,0:T(8,128)(2,1)S(1)}, bf16[128,1024]{1,0:T(8,128)(2,1)S(1)}, u32[]{:S(2)}, u32[]{:S(2)}) collective-permute-start(bf16[128,1024]{1,0:T(8,128)(2,1)S(1)} %slice.23), channel_id=1, source_target_pairs={{0,1},{1,0},{2,3},{3,2},{4,5},{5,4},{6,7},{7,6},{8,9},{9,8},{10,11... | collective-permute-start | bytes 786440 | tf_op jit(solution)/shard_map/ppermute | solution.py:1204
  180.1 10.4 %copy-start.10 = (f32[2,1024,4]{1,2,0:T(4,128)S(1)}, f32[2,1024,4]{1,2,0:T(4,128)}, u32[]{:S(2)}) copy-start(f32[2,1024,4]{1,2,0:T(4,128)} %param.30) | copy-start | bytes 98308
  180.1 10.4 %copy-start.11 = (f32[2,4,1024]{2,1,0:T(4,128)S(1)}, f32[2,4,1024]{2,1,0:T(4,128)}, u32[]{:S(2)}) copy-start(f32[2,4,1024]{2,1,0:T(4,128)} %mu_ref.1) | copy-start | bytes 98308
  180.1 10.4 %copy-start.12 = (f32[2,1024,4]{1,2,0:T(4,128)S(1)}, f32[2,1024,4]{1,2,0:T(4,128)}, u32[]{:S(2)}) copy-start(f32[2,1024,4]{1,2,0:T(4,128)} %param.32) | copy-start | bytes 98308
  180.1 10.4 %copy-start.13 = (f32[2,4,1024]{2,1,0:T(4,128)S(1)}, f32[2,4,1024]{2,1,0:T(4,128)}, u32[]{:S(2)}) copy-start(f32[2,4,1024]{2,1,0:T(4,128)} %au_ref.1) | copy-start | bytes 98308
  180.1 4.7 %collective-permute-start.26 = (f32[24,1024]{1,0:T(8,128)S(1)}, f32[24,1024]{1,0:T(8,128)S(1)}, u32[]{:S(2)}, u32[]{:S(2)}) collective-permute-start(f32[24,1024]{1,0:T(8,128)S(1)} %add.50), channel_id=1, source_target_pairs={{0,8},{1,9},{2,10},{3,11},{4,12},{5,13},{6,14},{7,15},{8,0},{9,1},... | collective-permute-start | bytes 294920 | tf_op jit(solution)/shard_map/ppermute | solution.py:1204
  184.8 5.6 %collective-permute-start.27 = (f32[24,1024]{1,0:T(8,128)S(1)}, f32[24,1024]{1,0:T(8,128)S(1)}, u32[]{:S(2)}, u32[]{:S(2)}) collective-permute-start(f32[24,1024]{1,0:T(8,128)S(1)} %add.51), channel_id=1, source_target_pairs={{0,16},{1,17},{2,18},{3,19},{4,20},{5,21},{6,22},{7,23},{8,24},{9,... | collective-permute-start | bytes 294920 | tf_op jit(solution)/shard_map/ppermute | solution.py:1204
